TPU v7x, 256 devices: a whole 4x4x8 slice. The times are simulated.
256 devices in a mesh: pipe: 8 (over y, core), space: 32 (over x, z).
Axes of the slice: x: 4, y: 4, z: 8, core: 2. Of those that a mesh axis runs over, the one named last changes fastest.
Arguments:
- activations: bfloat16 [8, 64, 128, 2048], P('pipe', 'space'), may hold values from -6 to 6
- cotangent: bfloat16 [64, 128, 2048], P('space'), may hold values from -6 to 6
- w_first: bfloat16 [8, 2, 8, 256, 256], P('pipe'), may hold values from -0.25 to 0.25
- w_second: bfloat16 [8, 2, 8, 256, 256], P('pipe'), may hold values from -0.25 to 0.25
- b_first: float32 [8, 2, 2048], P('pipe'), may hold values from -1 to 1
Outputs:
- grads: bfloat16 [8, 64, 128, 2048], P('pipe', 'space')
All inputs are finite; a program needn't handle non-finite values.
Results may differ from a plain program's by a relative error of at most 0.028.
Values may be sent and summed in bfloat16 or wider, within the bound.
No kernel may reach another device: no remote copies, remote signals or barrier semaphores. Data moves between devices by JAX's collectives and lax.ppermute only.
A program may use at most 64 MiB of HBM per device.

v0:
```python
import math

import jax
import jax.numpy as jnp
import numpy as np
from jax import lax
from jax.experimental import pallas as pl
from jax.experimental.pallas import tpu as pltpu
from jax.sharding import Mesh
from jax.sharding import PartitionSpec as P


BF16 = jnp.bfloat16
F32 = jnp.float32
X, Y, Z = 4, 4, 8
SMALL = pltpu.CompilerParams(vmem_limit_bytes=20 << 20)
TIGHT = pltpu.CompilerParams(vmem_limit_bytes=20 << 20)
EVERYONE = ("z", "core", "x", "y")


def rounded(table):
    return table.astype(np.float32).astype(BF16)


def row_matrix(rows, width, columns):
    modes = width // 2
    pair = modes // columns
    angles = 2.0 * math.pi * (np.outer(np.arange(modes), np.arange(width)) % width) / width
    scale = 1.0 / math.sqrt(width)
    parts = np.stack([np.cos(angles), -np.sin(angles)]) * scale
    table = np.zeros((columns, rows, 2, pair, rows, width))
    by_column = parts.reshape(2, columns, pair, width).transpose(1, 0, 2, 3)
    for h in range(rows):
        table[:, h, :, :, h, :] = by_column
    return table.reshape(columns * rows * 2 * pair, rows * width)


def column_matrix(height, pair):
    angles = 2.0 * math.pi * (np.outer(np.arange(height), np.arange(height)) % height) / height
    scale = 1.0 / math.sqrt(height)
    cosines, sines = np.cos(angles) * scale, np.sin(angles) * scale
    table = np.zeros((2, pair, height, height, 2, pair))
    for k in range(pair):
        table[0, k, :, :, 0, k] = cosines
        table[0, k, :, :, 1, k] = sines
        table[1, k, :, :, 1, k] = cosines
        table[1, k, :, :, 0, k] = -sines
    return table.reshape(2 * pair * height, 2 * pair * height)


def fold_matrices(height, pair):
    size = 2 * pair * height
    plain = np.eye(size)
    folded = np.eye(size).reshape(2, pair, height, 2, pair, height)
    eye = np.eye(height)
    flip = eye[(-np.arange(height)) % height]
    folded[0, 0, :, 0, 0, :] = 0.5 * (eye + flip)
    folded[1, 0, :, 1, 0, :] = 0.5 * (eye - flip)
    return np.stack([plain, folded.reshape(size, size)]).astype(np.float32).astype(BF16)


def dot(left, right):
    return jnp.dot(left, right, preferred_element_type=F32)


def dot_t(left, right):
    return lax.dot_general(left, right, (((1,), (1,)), ((), ())), preferred_element_type=F32)


def gelu_slope(values):
    return (
        0.5 * (1.0 + lax.erf(values * 0.7071067811865476))
        + values * jnp.exp(-0.5 * values * values) * 0.3989422804014327
    )


def first_kernel(table_hbm, act_hbm, cot_hbm, first_ref, second_ref, bias_hbm, *rest):
    pieces, cot_rows_ref, rows_ref = rest[:Y], rest[Y], rest[Y + 1]
    part, field, table_ref, act_ref, held, biases, sems, own_sems = rest[Y + 2 :]
    size = held.shape[2]
    y, core, z, odd = (*(lax.axis_index(name) for name in ("y", "core", "z")), lax.axis_index("x") & 1)
    target = (z + y + 4 * core) & (Z - 1)
    lines = part.shape[0]
    pairs = [
        (table_hbm.at[pl.ds(target * lines, lines)], part),
        (cot_hbm, field),
        (table_hbm, table_ref),
        (act_hbm, act_ref),
        (bias_hbm, biases),
    ]
    own = []
    for k, (source, place) in enumerate(pairs):
        copy = pltpu.make_async_copy(source, place, own_sems.at[k])
        copy.start()
        own.append(copy)
        if k != 1:
            continue
        loads = []
        for d in range(Y):
            block = ((y + d) & (Y - 1)) * 2 + odd
            for i in range(2):
                for j, ref in enumerate((first_ref, second_ref)):
                    copy = pltpu.make_async_copy(
                        ref.at[0, i, block],
                        held.at[d, pl.ds((2 * j + i) * size, size)],
                        sems.at[d, 2 * j + i],
                    )
                    copy.start()
                    loads.append(copy)

    line = lax.broadcasted_iota(jnp.int32, (lines, size), 0)
    zero_mode = jnp.logical_and(jnp.logical_and(line < 8, (line & 1) == 0), target == 0)
    factor = jnp.where(zero_mode, 1.0, 2.0).astype(F32)
    for copy in own[:2]:
        copy.wait()
    for n in range(2 * Y):
        tiles = (dot(part[...], field[:, n * size : (n + 1) * size]) * factor).astype(BF16)
        for i in range(2):
            for m in range(2):
                cot_rows_ref[i, n // 2, 2 * m + n % 2] = tiles[(2 * i + m) * 8 : (2 * i + m + 1) * 8]

    for copy in own[2:]:
        copy.wait()
    for d in range(Y):
        block = ((y + d) & (Y - 1)) * 2 + odd
        bias = biases[0, :, pl.ds(block * size, size)]
        high = bias.astype(BF16).astype(F32)
        middle = (bias - high).astype(BF16).astype(F32)
        low = bias - high - middle
        packed = jnp.concatenate([high, middle, low, jnp.zeros((10, size), F32)], axis=0)
        held[d, 4 * size : 4 * size + 16] = packed.astype(BF16)
    for copy in loads:
        copy.wait()
    stores = []
    for d in range(Y):
        copy = pltpu.make_async_copy(held.at[d], pieces[d], sems.at[d, 4])
        copy.start()
        stores.append(copy)
    for n in range(2 * Y):
        spectrum = dot(table_ref[...], act_ref[:, n * size : (n + 1) * size]).astype(BF16)
        rows_ref[:, :, :, n % 2, n // 2] = spectrum.reshape(Z, 2, 2, 8, size)
    for copy in stores:
        copy.wait()


def turn_core_kernel(arrived_ref, kept_ref, sent_ref):
    core = lax.axis_index("core")
    kept_ref[...] = arrived_ref[core]
    sent_ref[...] = arrived_ref[1 - core]


def turn_x_kernel(kept_ref, arrived_ref, *outs):
    x, core = lax.axis_index("x"), lax.axis_index("core")
    for e in range(X):
        to = (x + e) & (X - 1)
        outs[e][core] = kept_ref[:, to]
        outs[e][1 - core] = arrived_ref[:, to]


def turn_y_kernel(*refs):
    arrived, outs = refs[:X], refs[X:]
    y = lax.axis_index("y")
    for d in range(Y):
        for e in range(X):
            outs[d][e] = arrived[e][:, (y + d) & (Y - 1)]


def inverse_kernel(table_ref, spec_ref, cot_ref, out_ref, result, sems):
    rows = table_ref.shape[0]
    size = spec_ref.shape[6]
    copies = []
    for n in range(2 * Y):
        block = slice(n * size, (n + 1) * size)
        field = dot(table_ref[...], spec_ref[:, :, :, n % 2, n // 2].reshape(rows, size))
        result[:, block] = (field + cot_ref[:, block].astype(F32)).astype(BF16)
        copy = pltpu.make_async_copy(result.at[:, block], out_ref.at[:, block], sems.at[n])
        copy.start()
        copies.append(copy)
    for copy in copies:
        copy.wait()


def chain_kernel(act_ref, col_ref, inv_ref, fold_ref, *rest):
    sections = 2 * Y
    cots, weights = rest[:X], rest[X : X + sections]
    out_ref, found, held, sems = rest[X + sections :]
    size = act_ref.shape[6]
    half = col_ref.shape[0] // 2
    y, core, x, z = (lax.axis_index(name) for name in ("y", "core", "x", "z"))

    def load(p, source):
        return pltpu.make_async_copy(weights[source], held.at[p], sems.at[p])

    for here in range(sections):

        @pl.when(y * 2 + core == here)
        def _():
            for p in range(sections - 1, -1, -1):
                load(p, 2 * ((here // 2 - p // 2) % Y) + (p % 2 != here % 2)).start()

    for d in range(Y):
        for e in range(X):
            for i in range(2):
                found[(z - ((y - d) & (Y - 1)) - 4 * i) & (Z - 1), (x - e) & (X - 1)] = cots[d][e, i]
    has_zero = jnp.logical_and(jnp.logical_and(core == 0, x < 2), z == 0)
    fold = jnp.where(has_zero, 1, 0)

    base = dot(col_ref[...], found[...].reshape(2 * half, size))
    total = jnp.zeros_like(base)
    height_total = jnp.zeros_like(base)
    grad = base.astype(BF16)
    spectra = []
    for p in range(sections):
        columns = act_ref[:, p % 2, :, :, p // 2].reshape(2 * half, size)
        spectra.append(dot(col_ref[...], columns).astype(BF16))

    for p in range(sections - 1, -1, -1):
        load(p, 0).wait()
        a_re, a_im = held[p, 0:size], held[p, size : 2 * size]
        b_re, b_im = held[p, 2 * size : 3 * size], held[p, 3 * size : 4 * size]
        bias = held[p, 4 * size : 4 * size + 16].astype(F32)
        bias_re = bias[0:1] + bias[2:3] + bias[4:5]
        bias_im = bias[1:2] + bias[3:4] + bias[5:6]
        s = spectra[p]
        s_turned = jnp.concatenate([-s[half:], s[:half]], axis=0)
        z_both = dot(s, a_re) + dot(s_turned, a_im)
        slope = gelu_slope(jnp.concatenate([z_both[:half] + bias_re, z_both[half:] + bias_im], axis=0))
        g_turned = jnp.concatenate([grad[half:], -grad[:half]], axis=0)
        u = dot_t(grad, b_re) + dot_t(g_turned, b_im)
        q = (u * slope).astype(BF16)
        q_turned = jnp.concatenate([q[half:], -q[:half]], axis=0)
        e = (dot_t(q, a_re) + dot_t(q_turned, a_im)).astype(BF16)
        height_total = height_total + dot(inv_ref[...], e)
        out_ref[:, p % 2, :, :, p // 2] = height_total.astype(BF16).reshape(Z, 2, 2, 8, size)
        if p > 0:
            total = total + dot(fold_ref[fold], e)
            grad = (base + total).astype(BF16)


def body(activations, cotangent, w_first, w_second, b_first):
    sections, columns = 2 * Y, X * Z
    _, rows, width, channels = activations.shape
    size = w_first.shape[3]
    height = rows * columns
    pair = width // 2 // columns
    count = rows * width
    tile = 2 * rows * pair
    row_table = row_matrix(rows, width, columns)
    row_table = row_table.reshape(2, 2, Z, -1).transpose(2, 0, 1, 3).reshape(row_table.shape)
    forward_rows, inverse_rows = rounded(row_table), rounded(row_table.T)
    column_table = column_matrix(height, pair)
    column_table = column_table.reshape(-1, X, Z, tile).transpose(0, 2, 1, 3).reshape(column_table.shape)
    forward_columns, inverse_columns = rounded(column_table), rounded(column_table.T)
    folds = fold_matrices(height, pair)

    vmem = pl.BlockSpec(memory_space=pltpu.VMEM)
    hbm = pl.BlockSpec(memory_space=pl.ANY)
    blocks = (Z, 2, 2, 2, Y, tile, size)

    def shaped(*dims):
        return pltpu.VMEM(dims, BF16)

    def near(*values):
        return [pltpu.with_memory_space_constraint(value, pltpu.VMEM) for value in values]

    def far(*values):
        return [pltpu.with_memory_space_constraint(value, pltpu.HBM) for value in values]

    def exchange(value):
        flat = value.reshape(sections * columns, tile, size)
        return lax.all_to_all(flat, EVERYONE, split_axis=0, concat_axis=0, tiled=True).reshape(blocks)

    def shifted(value, axis, distance):
        size = lax.axis_size(axis)
        return lax.ppermute(value, axis, [(i, (i + distance) % size) for i in range(size)])

    flat_cot = cotangent.reshape(count, channels)
    made = pl.pallas_call(
        first_kernel,
        in_specs=[hbm] * 6,
        out_specs=[hbm] * Y + [vmem] * 2,
        out_shape=[pltpu.HBM((4 * size + 16, size), BF16)] * Y + [shaped(2, Y, X, tile, size), shaped(*blocks)],
        scratch_shapes=[
            pltpu.VMEM((4 * tile, count), BF16),
            pltpu.VMEM((count, channels), BF16),
            pltpu.VMEM(forward_rows.shape, BF16),
            pltpu.VMEM((count, channels), BF16),
            pltpu.VMEM((Y, 4 * size + 16, size), BF16),
            pltpu.VMEM(b_first.shape, F32),
            pltpu.SemaphoreType.DMA((Y, 5)),
            pltpu.SemaphoreType.DMA((5,)),
        ],
        compiler_params=SMALL,
        name="first",
    )(
        *far(
            jnp.asarray(forward_rows),
            activations.reshape(count, channels),
            flat_cot,
            w_first,
            w_second,
            b_first,
        )
    )
    pieces, cot_rows, act_rows = made[:Y], made[Y], made[Y + 1]
    route = []
    for line in range(2 * Y):
        shift = line // 2 + 4 * (line % 2)
        route += [(line * Z + z, line * Z + (z + shift) % Z) for z in range(Z)]
    arrived = lax.ppermute(cot_rows, ("y", "core", "z"), route)
    weights = []
    for d in range(Y):
        piece = shifted(pieces[d], "y", d) if d else pieces[0]
        weights += [piece, shifted(piece, "core", 1)]
    act_columns = exchange(act_rows)
    kept, sent = pl.pallas_call(
        turn_core_kernel,
        in_specs=[vmem],
        out_specs=[vmem] * 2,
        out_shape=[shaped(Y, X, tile, size)] * 2,
        compiler_params=SMALL,
        name="turn_core",
    )(*near(arrived))
    arrived = shifted(sent, "core", 1)
    turned = pl.pallas_call(
        turn_x_kernel,
        in_specs=[vmem] * 2,
        out_specs=[vmem] * X,
        out_shape=[shaped(2, Y, tile, size)] * X,
        compiler_params=SMALL,
        name="turn_x",
    )(*near(kept, arrived))
    arrived = [turned[0]] + [shifted(turned[e], "x", e) for e in range(1, X)]
    turned = pl.pallas_call(
        turn_y_kernel,
        in_specs=[vmem] * X,
        out_specs=[vmem] * Y,
        out_shape=[shaped(X, 2, tile, size)] * Y,
        compiler_params=SMALL,
        name="turn_y",
    )(*near(*arrived))
    cots = [turned[0]] + [shifted(turned[d], "y", d) for d in range(1, Y)]

    tables = [jnp.asarray(table) for table in (forward_columns, inverse_columns, folds)]
    back = pl.pallas_call(
        chain_kernel,
        in_specs=[vmem] * (4 + X) + [hbm] * sections,
        out_specs=vmem,
        out_shape=shaped(*blocks),
        scratch_shapes=[
            pltpu.VMEM((Z, X, tile, size), BF16),
            pltpu.VMEM((sections, 4 * size + 16, size), BF16),
            pltpu.SemaphoreType.DMA((sections,)),
        ],
        compiler_params=TIGHT,
        name="chain",
    )(*near(act_columns, *tables, *cots), *far(*weights))
    grads = pl.pallas_call(
        inverse_kernel,
        in_specs=[vmem] * 3,
        out_specs=hbm,
        out_shape=jax.ShapeDtypeStruct((count, channels), BF16),
        scratch_shapes=[pltpu.VMEM((count, channels), BF16), pltpu.SemaphoreType.DMA((sections,))],
        compiler_params=SMALL,
        name="inverse_rows",
    )(*near(jnp.asarray(inverse_rows), exchange(back), flat_cot))
    return grads.reshape(1, rows, width, channels)


def solution(mesh):
    chips = Mesh(mesh.devices.reshape(Y, 2, X, Z), ("y", "core", "x", "z"))
    pipe, space = ("y", "core"), ("x", "z")
    in_specs = (
        P(pipe, space, None, None),
        P(space, None, None),
        P(pipe, None, None, None, None),
        P(pipe, None, None, None, None),
        P(pipe, None, None),
    )
    out_specs = P(pipe, space, None, None)
    return jax.shard_map(body, mesh=chips, in_specs=in_specs, out_specs=out_specs, check_vma=False)
```

profile of v0, /device:TPU:1, one launch (start us, length us, event | category | flops | bytes accessed | tf_op | source)
XLA Modules:
  0.0 152.5 jit_solution(18258590465967953570)
XLA Ops:
  0.0 4.9 %first.1 = (bf16[1040,256]{1,0:T(8,128)(2,1)}, bf16[1040,256]{1,0:T(8,128)(2,1)}, bf16[1040,256]{1,0:T(8,128)(2,1)}, bf16[1040,256]{1,0:T(8,128)(2,1)}, bf16[2,4...) custom-call(bf16[256,256]{1,0:T(8,128)(2,1)} %constant.10.clone.table_hbm, ...), custom_call_target="tpu_custom_call" | custom-call | tf_op jit(solution)/shard_map/first/pallas_call | solution.py:278
  4.9 15.7 %all-to-all-start = ((bf16[256,8,256]{2,1,0:T(8,128)(2,1)}), bf16[256,8,256]{2,1,0:T(8,128)(2,1)S(1)}, u32[]{:S(2)}, u32[]{:S(2)}) async-start(bf16[256,8,256]{2,1,0:T(8,128)(2,1)} %bitcast.2), calls=%async_computation | async-start | bytes 2097152 | tf_op jit(solution)/shard_map/all_to_all | solution.py:271
  20.6 1.4 collective-permute-start.9
  22.0 2.5 %collective-permute-start.11 = (bf16[1040,256]{1,0:T(8,128)(2,1)}, bf16[1040,256]{1,0:T(8,128)(2,1)S(1)}, u32[]{:S(2)}, u32[]{:S(2)}) collective-permute-start(bf16[1040,256]{1,0:T(8,128)(2,1)} %get-tuple-element.35), channel_id=1, source_target_pairs={{0,128},{64,192},{128,0},{192,64},{1,129},{65,193},{129,1},{193,65... | collective-permute-start | bytes 1597448 | tf_op jit(solution)/shard_map/ppermute | solution.py:275
  24.5 1.1 collective-permute-start.13
  25.6 1.2 collective-permute-start.8
  26.9 15.3 %collective-permute-done.9.rest_6_ = bf16[1040,256]{1,0:T(8,128)(2,1)S(1)} collective-permute-done((bf16[1040,256]{1,0:T(8,128)(2,1)}, bf16[1040,256]{1,0:T(8,128)(2,1)S(1)}, u32[]{:S(2)}, u32[]{:S(2)}) %collective-permute-start.9) | collective-permute-done | bytes 532512 | tf_op jit(solution)/shard_map/ppermute | solution.py:275
  42.2 3.1 %collective-permute-start.10 = (bf16[1040,256]{1,0:T(8,128)(2,1)S(1)}, bf16[1040,256]{1,0:T(8,128)(2,1)S(1)}, u32[]{:S(2)}, u32[]{:S(2)}) collective-permute-start(bf16[1040,256]{1,0:T(8,128)(2,1)S(1)} %collective-permute-done.9.rest_6_), channel_id=1, source_target_pairs={{0,32},{32,0},{1,33},{33,1},{2,34},{34,2},{3,35},{35,3},{4,36},{36... | collective-permute-start | bytes 1597448 | tf_op jit(solution)/shard_map/ppermute | solution.py:275
  45.2 13.4 %collective-permute-done.11.rest_8_ = bf16[1040,256]{1,0:T(8,128)(2,1)S(1)} collective-permute-done((bf16[1040,256]{1,0:T(8,128)(2,1)}, bf16[1040,256]{1,0:T(8,128)(2,1)S(1)}, u32[]{:S(2)}, u32[]{:S(2)}) %collective-permute-start.11) | collective-permute-done | bytes 532512 | tf_op jit(solution)/shard_map/ppermute | solution.py:275
  58.6 0.9 collective-permute-start.12
  59.7 7.4 %collective-permute-start = (bf16[2,4,4,8,256]{4,3,2,1,0:T(8,128)(2,1)S(1)}, bf16[2,4,4,8,256]{4,3,2,1,0:T(8,128)(2,1)S(1)}, u32[]{:S(2)}, u32[]{:S(2)}) collective-permute-start(bf16[2,4,4,8,256]{4,3,2,1,0:T(8,128)(2,1)S(1)} %get-tuple-element.22), channel_id=1, source_target_pairs={{0,0},{1,1},{2,2},{3,3},{4,4},{5,5},{6,6},{7,7},{32,36},{33,37},{3... | collective-permute-start | bytes 393224 | tf_op jit(solution)/shard_map/ppermute | solution.py:310
  67.0 2.4 %collective-permute-done.arrived_ref = bf16[2,4,4,8,256]{4,3,2,1,0:T(8,128)(2,1)S(1)} collective-permute-done((bf16[2,4,4,8,256]{4,3,2,1,0:T(8,128)(2,1)S(1)}, bf16[2,4,4,8,256]{4,3,2,1,0:T(8,128)(2,1)S(1)}, u32[]{:S(2)}, u32[]{:S(2)}) %collective-permute-start) | collective-permute-done | bytes 131104 | tf_op jit(solution)/shard_map/ppermute | solution.py:310
  69.6 1.2 collective-permute-done.1.arrived_ref
  71.6 3.3 %collective-permute-done.2.refs_1_ = bf16[2,4,8,256]{3,2,1,0:T(8,128)(2,1)S(1)} collective-permute-done((bf16[2,4,8,256]{3,2,1,0:T(8,128)(2,1)S(1)}, bf16[2,4,8,256]{3,2,1,0:T(8,128)(2,1)S(1)}, u32[]{:S(2)}, u32[]{:S(2)}) %collective-permute-start.2) | collective-permute-done | bytes 32800 | tf_op jit(solution)/shard_map/ppermute | solution.py:275
  75.6 3.6 %collective-permute-done.3.refs_2_ = bf16[2,4,8,256]{3,2,1,0:T(8,128)(2,1)S(1)} collective-permute-done((bf16[2,4,8,256]{3,2,1,0:T(8,128)(2,1)S(1)}, bf16[2,4,8,256]{3,2,1,0:T(8,128)(2,1)S(1)}, u32[]{:S(2)}, u32[]{:S(2)}) %collective-permute-start.3) | collective-permute-done | bytes 32800 | tf_op jit(solution)/shard_map/ppermute | solution.py:275
  79.6 2.3 %collective-permute-done.4.refs_3_ = bf16[2,4,8,256]{3,2,1,0:T(8,128)(2,1)S(1)} collective-permute-done((bf16[2,4,8,256]{3,2,1,0:T(8,128)(2,1)S(1)}, bf16[2,4,8,256]{3,2,1,0:T(8,128)(2,1)S(1)}, u32[]{:S(2)}, u32[]{:S(2)}) %collective-permute-start.4) | collective-permute-done | bytes 32800 | tf_op jit(solution)/shard_map/ppermute | solution.py:275
  82.0 1.8 %collective-permute-start.5 = (bf16[4,2,8,256]{3,2,1,0:T(8,128)(2,1)S(1)}, bf16[4,2,8,256]{3,2,1,0:T(8,128)(2,1)S(1)}, u32[]{:S(2)}, u32[]{:S(2)}) collective-permute-start(bf16[4,2,8,256]{3,2,1,0:T(8,128)(2,1)S(1)} %get-tuple-element.30), channel_id=1, source_target_pairs={{0,64},{64,128},{128,192},{192,0},{1,65},{65,129},{129,193},{193,1... | collective-permute-start | bytes 98312 | tf_op jit(solution)/shard_map/ppermute | solution.py:275
  83.8 2.3 %collective-permute-done.5.rest_1_ = bf16[4,2,8,256]{3,2,1,0:T(8,128)(2,1)S(1)} collective-permute-done((bf16[4,2,8,256]{3,2,1,0:T(8,128)(2,1)S(1)}, bf16[4,2,8,256]{3,2,1,0:T(8,128)(2,1)S(1)}, u32[]{:S(2)}, u32[]{:S(2)}) %collective-permute-start.5) | collective-permute-done | bytes 32800 | tf_op jit(solution)/shard_map/ppermute | solution.py:275
  86.0 0.8 collective-permute-start.6
  86.8 3.6 %collective-permute-done.6.rest_2_ = bf16[4,2,8,256]{3,2,1,0:T(8,128)(2,1)S(1)} collective-permute-done((bf16[4,2,8,256]{3,2,1,0:T(8,128)(2,1)S(1)}, bf16[4,2,8,256]{3,2,1,0:T(8,128)(2,1)S(1)}, u32[]{:S(2)}, u32[]{:S(2)}) %collective-permute-start.6) | collective-permute-done | bytes 32800 | tf_op jit(solution)/shard_map/ppermute | solution.py:275
  90.5 2.8 %collective-permute-done.7.rest_3_ = bf16[4,2,8,256]{3,2,1,0:T(8,128)(2,1)S(1)} collective-permute-done((bf16[4,2,8,256]{3,2,1,0:T(8,128)(2,1)S(1)}, bf16[4,2,8,256]{3,2,1,0:T(8,128)(2,1)S(1)}, u32[]{:S(2)}, u32[]{:S(2)}) %collective-permute-start.7) | collective-permute-done | bytes 32800 | tf_op jit(solution)/shard_map/ppermute | solution.py:275
  95.2 8.1 %chain.1 = bf16[8,2,2,2,4,8,256]{6,5,4,3,2,1,0:T(8,128)(2,1)S(1)} custom-call(bf16[8,2,2,2,4,8,256]{6,5,4,3,2,1,0:T(8,128)(2,1)S(1)} %bitcast.10, bf16[256,256]{1,0:T(8,128)(2,1)S(1)} %copy-done.4, bf16[256,256]{1,0:T(8,128)(2,1)S(1)} %copy-done.3, bf16[2,256,256]{2,1,0:T(8,128)(2,1)S(1)} %copy-done.1, bf16[4,2,8,256]{3,2,1,0:T(8,128)(2,1)S(1)} %get-tuple-element.29.rest_0_, ...), custom_call_target="tpu_custom_call" | custom-call | tf_op jit(solution)/shard_map/chain/pallas_call | solution.py:345
  103.3 47.7 %all_to_all.10 = bf16[256,8,256]{2,1,0:T(8,128)(2,1)S(1)} all-to-all(bf16[256,8,256]{2,1,0:T(8,128)(2,1)S(1)} %bitcast.11), channel_id=1, replica_groups=mesh['y'=4,'core'=2,'x'=4,'z'=8] {'z','core','x','y'}, dimensions={0} | all-to-all | bytes 2097152 | tf_op jit(solution)/shard_map/all_to_all | solution.py:271
  151.1 1.3 inverse_rows.1
  (39 shorter events, 4.1 us)
Async XLA Ops:
  4.9 90.2 %copy-start.1 = (bf16[2,256,256]{2,1,0:T(8,128)(2,1)S(1)}, bf16[2,256,256]{2,1,0:T(8,128)(2,1)}, u32[]{:S(2)}) copy-start(bf16[2,256,256]{2,1,0:T(8,128)(2,1)} %constant.13.clone.fold_ref) | copy-start | bytes 786436
  4.9 90.2 %copy-start.3 = (bf16[256,256]{1,0:T(8,128)(2,1)S(1)}, bf16[256,256]{1,0:T(8,128)(2,1)}, u32[]{:S(2)}) copy-start(bf16[256,256]{1,0:T(8,128)(2,1)} %constant.12.clone.inv_ref) | copy-start | bytes 393220
  4.9 90.2 %copy-start.4 = (bf16[256,256]{1,0:T(8,128)(2,1)S(1)}, bf16[256,256]{1,0:T(8,128)(2,1)}, u32[]{:S(2)}) copy-start(bf16[256,256]{1,0:T(8,128)(2,1)} %constant.11.clone.col_ref) | copy-start | bytes 393220
  4.9 90.2 %all-to-all-start = ((bf16[256,8,256]{2,1,0:T(8,128)(2,1)}), bf16[256,8,256]{2,1,0:T(8,128)(2,1)S(1)}, u32[]{:S(2)}, u32[]{:S(2)}) async-start(bf16[256,8,256]{2,1,0:T(8,128)(2,1)} %bitcast.2), calls=%async_computation | async-start | bytes 2097152 | tf_op jit(solution)/shard_map/all_to_all | solution.py:271
  20.6 21.5 %collective-permute-start.9 = (bf16[1040,256]{1,0:T(8,128)(2,1)}, bf16[1040,256]{1,0:T(8,128)(2,1)S(1)}, u32[]{:S(2)}, u32[]{:S(2)}) collective-permute-start(bf16[1040,256]{1,0:T(8,128)(2,1)} %get-tuple-element.34), channel_id=1, source_target_pairs={{0,64},{64,128},{128,192},{192,0},{1,65},{65,129},{129,193},{193,1... | collective-permute-start | bytes 1597448 | tf_op jit(solution)/shard_map/ppermute | solution.py:275
  22.0 36.6 %collective-permute-start.11 = (bf16[1040,256]{1,0:T(8,128)(2,1)}, bf16[1040,256]{1,0:T(8,128)(2,1)S(1)}, u32[]{:S(2)}, u32[]{:S(2)}) collective-permute-start(bf16[1040,256]{1,0:T(8,128)(2,1)} %get-tuple-element.35), channel_id=1, source_target_pairs={{0,128},{64,192},{128,0},{192,64},{1,129},{65,193},{129,1},{193,65... | collective-permute-start | bytes 1597448 | tf_op jit(solution)/shard_map/ppermute | solution.py:275
  24.5 35.1 %collective-permute-start.13 = (bf16[1040,256]{1,0:T(8,128)(2,1)}, bf16[1040,256]{1,0:T(8,128)(2,1)S(1)}, u32[]{:S(2)}, u32[]{:S(2)}) collective-permute-start(bf16[1040,256]{1,0:T(8,128)(2,1)} %get-tuple-element.36), channel_id=1, source_target_pairs={{0,192},{64,0},{128,64},{192,128},{1,193},{65,1},{129,65},{193,129... | collective-permute-start | bytes 1597448 | tf_op jit(solution)/shard_map/ppermute | solution.py:275
  25.6 67.7 %collective-permute-start.8 = (bf16[1040,256]{1,0:T(8,128)(2,1)S(1)}, bf16[1040,256]{1,0:T(8,128)(2,1)S(1)}, u32[]{:S(2)}, u32[]{:S(2)}) collective-permute-start(bf16[1040,256]{1,0:T(8,128)(2,1)S(1)} %copy-done.5), channel_id=1, source_target_pairs={{0,32},{32,0},{1,33},{33,1},{2,34},{34,2},{3,35},{35,3},{4,36},{36... | collective-permute-start | bytes 1597448 | tf_op jit(solution)/shard_map/ppermute | solution.py:275
  42.2 53.0 %copy-start.6 = (bf16[1040,256]{1,0:T(8,128)(2,1)}, bf16[1040,256]{1,0:T(8,128)(2,1)S(1)}, u32[]{:S(2)}) copy-start(bf16[1040,256]{1,0:T(8,128)(2,1)S(1)} %collective-permute-done.9.rest_6_) | copy-start | bytes 1597444
  42.2 51.2 %collective-permute-start.10 = (bf16[1040,256]{1,0:T(8,128)(2,1)S(1)}, bf16[1040,256]{1,0:T(8,128)(2,1)S(1)}, u32[]{:S(2)}, u32[]{:S(2)}) collective-permute-start(bf16[1040,256]{1,0:T(8,128)(2,1)S(1)} %collective-permute-done.9.rest_6_), channel_id=1, source_target_pairs={{0,32},{32,0},{1,33},{33,1},{2,34},{34,2},{3,35},{35,3},{4,36},{36... | collective-permute-start | bytes 1597448 | tf_op jit(solution)/shard_map/ppermute | solution.py:275
  58.6 36.5 %copy-start.7 = (bf16[1040,256]{1,0:T(8,128)(2,1)}, bf16[1040,256]{1,0:T(8,128)(2,1)S(1)}, u32[]{:S(2)}) copy-start(bf16[1040,256]{1,0:T(8,128)(2,1)S(1)} %collective-permute-done.11.rest_8_) | copy-start | bytes 1597444
  58.6 34.7 %collective-permute-start.12 = (bf16[1040,256]{1,0:T(8,128)(2,1)S(1)}, bf16[1040,256]{1,0:T(8,128)(2,1)S(1)}, u32[]{:S(2)}, u32[]{:S(2)}) collective-permute-start(bf16[1040,256]{1,0:T(8,128)(2,1)S(1)} %collective-permute-done.11.rest_8_), channel_id=1, source_target_pairs={{0,32},{32,0},{1,33},{33,1},{2,34},{34,2},{3,35},{35,3},{4,36},{36... | collective-permute-start | bytes 1597448 | tf_op jit(solution)/shard_map/ppermute | solution.py:275
  59.6 33.8 %copy-start.8 = (bf16[1040,256]{1,0:T(8,128)(2,1)}, bf16[1040,256]{1,0:T(8,128)(2,1)S(1)}, u32[]{:S(2)}) copy-start(bf16[1040,256]{1,0:T(8,128)(2,1)S(1)} %collective-permute-done.13.rest_10_) | copy-start | bytes 1597444
  59.6 35.6 %collective-permute-start.14 = (bf16[1040,256]{1,0:T(8,128)(2,1)S(1)}, bf16[1040,256]{1,0:T(8,128)(2,1)}, u32[]{:S(2)}, u32[]{:S(2)}) collective-permute-start(bf16[1040,256]{1,0:T(8,128)(2,1)S(1)} %collective-permute-done.13.rest_10_), channel_id=1, source_target_pairs={{0,32},{32,0},{1,33},{33,1},{2,34},{34,2},{3,35},{35,3},{4,36},{36... | collective-permute-start | bytes 1597448 | tf_op jit(solution)/shard_map/ppermute | solution.py:275
  59.7 9.8 %collective-permute-start = (bf16[2,4,4,8,256]{4,3,2,1,0:T(8,128)(2,1)S(1)}, bf16[2,4,4,8,256]{4,3,2,1,0:T(8,128)(2,1)S(1)}, u32[]{:S(2)}, u32[]{:S(2)}) collective-permute-start(bf16[2,4,4,8,256]{4,3,2,1,0:T(8,128)(2,1)S(1)} %get-tuple-element.22), channel_id=1, source_target_pairs={{0,0},{1,1},{2,2},{3,3},{4,4},{5,5},{6,6},{7,7},{32,36},{33,37},{3... | collective-permute-start | bytes 393224 | tf_op jit(solution)/shard_map/ppermute | solution.py:310
  69.5 1.3 collective-permute-start.1
  70.9 4.1 %collective-permute-start.2 = (bf16[2,4,8,256]{3,2,1,0:T(8,128)(2,1)S(1)}, bf16[2,4,8,256]{3,2,1,0:T(8,128)(2,1)S(1)}, u32[]{:S(2)}, u32[]{:S(2)}) collective-permute-start(bf16[2,4,8,256]{3,2,1,0:T(8,128)(2,1)S(1)} %get-tuple-element.26), channel_id=1, source_target_pairs={{0,8},{8,16},{16,24},{24,0},{1,9},{9,17},{17,25},{25,1},{2,10},{10... | collective-permute-start | bytes 98312 | tf_op jit(solution)/shard_map/ppermute | solution.py:275
  74.9 4.3 %collective-permute-start.3 = (bf16[2,4,8,256]{3,2,1,0:T(8,128)(2,1)S(1)}, bf16[2,4,8,256]{3,2,1,0:T(8,128)(2,1)S(1)}, u32[]{:S(2)}, u32[]{:S(2)}) collective-permute-start(bf16[2,4,8,256]{3,2,1,0:T(8,128)(2,1)S(1)} %get-tuple-element.27), channel_id=1, source_target_pairs={{0,16},{8,24},{16,0},{24,8},{1,17},{9,25},{17,1},{25,9},{2,18},{10... | collective-permute-start | bytes 98312 | tf_op jit(solution)/shard_map/ppermute | solution.py:275
  79.2 2.8 %collective-permute-start.4 = (bf16[2,4,8,256]{3,2,1,0:T(8,128)(2,1)S(1)}, bf16[2,4,8,256]{3,2,1,0:T(8,128)(2,1)S(1)}, u32[]{:S(2)}, u32[]{:S(2)}) collective-permute-start(bf16[2,4,8,256]{3,2,1,0:T(8,128)(2,1)S(1)} %get-tuple-element.28), channel_id=1, source_target_pairs={{0,24},{8,0},{16,8},{24,16},{1,25},{9,1},{17,9},{25,17},{2,26},{10... | collective-permute-start | bytes 98312 | tf_op jit(solution)/shard_map/ppermute | solution.py:275
  82.0 4.1 %collective-permute-start.5 = (bf16[4,2,8,256]{3,2,1,0:T(8,128)(2,1)S(1)}, bf16[4,2,8,256]{3,2,1,0:T(8,128)(2,1)S(1)}, u32[]{:S(2)}, u32[]{:S(2)}) collective-permute-start(bf16[4,2,8,256]{3,2,1,0:T(8,128)(2,1)S(1)} %get-tuple-element.30), channel_id=1, source_target_pairs={{0,64},{64,128},{128,192},{192,0},{1,65},{65,129},{129,193},{193,1... | collective-permute-start | bytes 98312 | tf_op jit(solution)/shard_map/ppermute | solution.py:275
  86.0 4.4 %collective-permute-start.6 = (bf16[4,2,8,256]{3,2,1,0:T(8,128)(2,1)S(1)}, bf16[4,2,8,256]{3,2,1,0:T(8,128)(2,1)S(1)}, u32[]{:S(2)}, u32[]{:S(2)}) collective-permute-start(bf16[4,2,8,256]{3,2,1,0:T(8,128)(2,1)S(1)} %get-tuple-element.31), channel_id=1, source_target_pairs={{0,128},{64,192},{128,0},{192,64},{1,129},{65,193},{129,1},{193,65... | collective-permute-start | bytes 98312 | tf_op jit(solution)/shard_map/ppermute | solution.py:275
  90.4 2.9 %collective-permute-start.7 = (bf16[4,2,8,256]{3,2,1,0:T(8,128)(2,1)S(1)}, bf16[4,2,8,256]{3,2,1,0:T(8,128)(2,1)S(1)}, u32[]{:S(2)}, u32[]{:S(2)}) collective-permute-start(bf16[4,2,8,256]{3,2,1,0:T(8,128)(2,1)S(1)} %get-tuple-element.32), channel_id=1, source_target_pairs={{0,192},{64,0},{128,64},{192,128},{1,193},{65,1},{129,65},{193,129... | collective-permute-start | bytes 98312 | tf_op jit(solution)/shard_map/ppermute | solution.py:275
  103.3 47.8 %copy-start = (bf16[2,128,2048]{2,1,0:T(8,128)(2,1)S(1)}, bf16[2,128,2048]{2,1,0:T(8,128)(2,1)}, u32[]{:S(2)}) copy-start(bf16[2,128,2048]{2,1,0:T(8,128)(2,1)} %param.11) | copy-start | bytes 3145732
  103.3 47.8 %copy-start.2 = (bf16[256,256]{1,0:T(8,128)(2,1)S(1)}, bf16[256,256]{1,0:T(8,128)(2,1)}, u32[]{:S(2)}) copy-start(bf16[256,256]{1,0:T(8,128)(2,1)} %constant.14.clone.table_ref) | copy-start | bytes 393220
  (4 other events, 23.3 us)
where the time goes:
time: 153 us; the launch traced here: 152 us
  waiting for transfers between devices  50.2 us (33%)
  blocking collectives  47.7 us (31%)
  starting transfers between devices  38.1 us (25%)
  Pallas kernels  14.3 us (9%)
  local copies, waits for them, and re-layouts  1.81 us (1%)
    ppermute x14, waiting for transfers between devices, shifted(): lax.ppermute(value, axis, [(i, (i + distance) % size) for i in range(size)])  47.8 us
    all_to_all x1, blocking collectives, exchange(): lax.all_to_all(flat, EVERYONE, split_axis=0, concat_axis=0, tiled=True)  47.7 us
    all_to_all x1, starting transfers between devices, exchange(): lax.all_to_all(flat, EVERYONE, split_axis=0, concat_axis=0, tiled=True)  15.7 us
    ppermute x14, starting transfers between devices, shifted(): lax.ppermute(value, axis, [(i, (i + distance) % size) for i in range(size)])  15 us
    pallas_call x1, Pallas kernels, body(): pl.pallas_call(chain_kernel, in_specs=[vmem] * (4 + X) + [hbm] * sections...  8.11 us
    ppermute x1, starting transfers between devices, body(): arrived = lax.ppermute(cot_rows, ('y', 'core', 'z'), route)  7.38 us
    pallas_call x1, Pallas kernels, body(): pl.pallas_call(first_kernel, in_specs=[hbm] * 6, out_specs=[hbm] * Y + [v...  4.89 us
  transfers between devices with their start and end apart: 16, of which 10 were waited for; matrix products, arithmetic and copies ran while one was open for 0% of the time, Pallas kernels for 0%

commit v1 on v0

--- a/solution.py
+++ b/solution.py
@@ -18,8 +18,10 @@
 EVERYONE = ("z", "core", "x", "y")
 
 
-def rounded(table):
-    return table.astype(np.float32).astype(BF16)
+def two_parts(table):
+    high = table.astype(np.float32).astype(BF16)
+    low = (table - high.astype(np.float64)).astype(np.float32).astype(BF16)
+    return np.concatenate([high, low], axis=1)
 
 
 def row_matrix(rows, width, columns):
@@ -72,6 +74,11 @@
         0.5 * (1.0 + lax.erf(values * 0.7071067811865476))
         + values * jnp.exp(-0.5 * values * values) * 0.3989422804014327
     )
+
+
+def twice(table_ref, operand):
+    depth = operand.shape[0]
+    return dot(table_ref[:, :depth], operand) + dot(table_ref[:, depth:], operand)
 
 
 def first_kernel(table_hbm, act_hbm, cot_hbm, first_ref, second_ref, bias_hbm, *rest):
@@ -93,34 +100,41 @@
         copy = pltpu.make_async_copy(source, place, own_sems.at[k])
         copy.start()
         own.append(copy)
-        if k != 1:
-            continue
-        loads = []
-        for d in range(Y):
-            block = ((y + d) & (Y - 1)) * 2 + odd
-            for i in range(2):
-                for j, ref in enumerate((first_ref, second_ref)):
-                    copy = pltpu.make_async_copy(
-                        ref.at[0, i, block],
-                        held.at[d, pl.ds((2 * j + i) * size, size)],
-                        sems.at[d, 2 * j + i],
-                    )
-                    copy.start()
-                    loads.append(copy)
-
+    loads = []
+    for d in range(Y):
+        block = ((y + d) & (Y - 1)) * 2 + odd
+        for i in range(2):
+            for j, ref in enumerate((first_ref, second_ref)):
+                copy = pltpu.make_async_copy(
+                    ref.at[0, i, block],
+                    held.at[d, pl.ds((2 * j + i) * size, size)],
+                    sems.at[d, 2 * j + i],
+                )
+                copy.start()
+                loads.append(copy)
+
+    depth = table_ref.shape[1] // 2
     line = lax.broadcasted_iota(jnp.int32, (lines, size), 0)
     zero_mode = jnp.logical_and(jnp.logical_and(line < 8, (line & 1) == 0), target == 0)
     factor = jnp.where(zero_mode, 1.0, 2.0).astype(F32)
     for copy in own[:2]:
         copy.wait()
+    rows = jnp.concatenate([part[:, :depth], part[:, depth:]], axis=0)
     for n in range(2 * Y):
-        tiles = (dot(part[...], field[:, n * size : (n + 1) * size]) * factor).astype(BF16)
+        spectrum = dot(rows, field[:, n * size : (n + 1) * size])
+        tiles = ((spectrum[:lines] + spectrum[lines:]) * factor).astype(BF16)
         for i in range(2):
             for m in range(2):
                 cot_rows_ref[i, n // 2, 2 * m + n % 2] = tiles[(2 * i + m) * 8 : (2 * i + m + 1) * 8]
 
+    def transform(n):
+        spectrum = twice(table_ref, act_ref[:, n * size : (n + 1) * size]).astype(BF16)
+        rows_ref[:, :, :, n % 2, n // 2] = spectrum.reshape(Z, 2, 2, 8, size)
+
     for copy in own[2:]:
         copy.wait()
+    for n in range(3):
+        transform(n)
     for d in range(Y):
         block = ((y + d) & (Y - 1)) * 2 + odd
         bias = biases[0, :, pl.ds(block * size, size)]
@@ -136,9 +150,8 @@
         copy = pltpu.make_async_copy(held.at[d], pieces[d], sems.at[d, 4])
         copy.start()
         stores.append(copy)
-    for n in range(2 * Y):
-        spectrum = dot(table_ref[...], act_ref[:, n * size : (n + 1) * size]).astype(BF16)
-        rows_ref[:, :, :, n % 2, n // 2] = spectrum.reshape(Z, 2, 2, 8, size)
+    for n in range(3, 2 * Y):
+        transform(n)
     for copy in stores:
         copy.wait()
 
@@ -171,7 +184,7 @@
     copies = []
     for n in range(2 * Y):
         block = slice(n * size, (n + 1) * size)
-        field = dot(table_ref[...], spec_ref[:, :, :, n % 2, n // 2].reshape(rows, size))
+        field = twice(table_ref, spec_ref[:, :, :, n % 2, n // 2].reshape(rows, size))
         result[:, block] = (field + cot_ref[:, block].astype(F32)).astype(BF16)
         copy = pltpu.make_async_copy(result.at[:, block], out_ref.at[:, block], sems.at[n])
         copy.start()
@@ -205,14 +218,14 @@
     has_zero = jnp.logical_and(jnp.logical_and(core == 0, x < 2), z == 0)
     fold = jnp.where(has_zero, 1, 0)
 
-    base = dot(col_ref[...], found[...].reshape(2 * half, size))
+    base = twice(col_ref, found[...].reshape(2 * half, size))
     total = jnp.zeros_like(base)
     height_total = jnp.zeros_like(base)
     grad = base.astype(BF16)
     spectra = []
     for p in range(sections):
         columns = act_ref[:, p % 2, :, :, p // 2].reshape(2 * half, size)
-        spectra.append(dot(col_ref[...], columns).astype(BF16))
+        spectra.append(twice(col_ref, columns).astype(BF16))
 
     for p in range(sections - 1, -1, -1):
         load(p, 0).wait()
@@ -230,7 +243,7 @@
         q = (u * slope).astype(BF16)
         q_turned = jnp.concatenate([q[half:], -q[:half]], axis=0)
         e = (dot_t(q, a_re) + dot_t(q_turned, a_im)).astype(BF16)
-        height_total = height_total + dot(inv_ref[...], e)
+        height_total = height_total + twice(inv_ref, e)
         out_ref[:, p % 2, :, :, p // 2] = height_total.astype(BF16).reshape(Z, 2, 2, 8, size)
         if p > 0:
             total = total + dot(fold_ref[fold], e)
@@ -247,10 +260,10 @@
     tile = 2 * rows * pair
     row_table = row_matrix(rows, width, columns)
     row_table = row_table.reshape(2, 2, Z, -1).transpose(2, 0, 1, 3).reshape(row_table.shape)
-    forward_rows, inverse_rows = rounded(row_table), rounded(row_table.T)
+    forward_rows, inverse_rows = two_parts(row_table), two_parts(row_table.T)
     column_table = column_matrix(height, pair)
     column_table = column_table.reshape(-1, X, Z, tile).transpose(0, 2, 1, 3).reshape(column_table.shape)
-    forward_columns, inverse_columns = rounded(column_table), rounded(column_table.T)
+    forward_columns, inverse_columns = two_parts(column_table), two_parts(column_table.T)
     folds = fold_matrices(height, pair)
 
     vmem = pl.BlockSpec(memory_space=pltpu.VMEM)
@@ -281,7 +294,7 @@
         out_specs=[hbm] * Y + [vmem] * 2,
         out_shape=[pltpu.HBM((4 * size + 16, size), BF16)] * Y + [shaped(2, Y, X, tile, size), shaped(*blocks)],
         scratch_shapes=[
-            pltpu.VMEM((4 * tile, count), BF16),
+            pltpu.VMEM((4 * tile, 2 * count), BF16),
             pltpu.VMEM((count, channels), BF16),
             pltpu.VMEM(forward_rows.shape, BF16),
             pltpu.VMEM((count, channels), BF16),

time: 153 us -> 154 us (level)
  no operation moved by 1% of the time
where the time goes in v1:
time: 154 us
  waiting for transfers between devices  50.2 us (33%)
  blocking collectives  47.7 us (31%)
  starting transfers between devices  38.1 us (25%)
  Pallas kernels  15.4 us (10%)
  local copies, waits for them, and re-layouts  1.8 us (1%)
    ppermute x14, waiting for transfers between devices, shifted(): lax.ppermute(value, axis, [(i, (i + distance) % size) for i in range(size)])  47.8 us
    all_to_all x1, blocking collectives, exchange(): lax.all_to_all(flat, EVERYONE, split_axis=0, concat_axis=0, tiled=True)  47.7 us
    all_to_all x1, starting transfers between devices, exchange(): lax.all_to_all(flat, EVERYONE, split_axis=0, concat_axis=0, tiled=True)  15.7 us
    ppermute x14, starting transfers between devices, shifted(): lax.ppermute(value, axis, [(i, (i + distance) % size) for i in range(size)])  15 us
    pallas_call x1, Pallas kernels, body(): pl.pallas_call(chain_kernel, in_specs=[vmem] * (4 + X) + [hbm] * sections...  8.47 us
    ppermute x1, starting transfers between devices, body(): arrived = lax.ppermute(cot_rows, ('y', 'core', 'z'), route)  7.38 us
    pallas_call x1, Pallas kernels, body(): pl.pallas_call(first_kernel, in_specs=[hbm] * 6, out_specs=[hbm] * Y + [v...  5.3 us
  transfers between devices with their start and end apart: 16, of which 10 were waited for; matrix products, arithmetic and copies ran while one was open for 0% of the time, Pallas kernels for 0%

profile of v1, /device:TPU:1, one launch (start us, length us, event | category | flops | bytes accessed | tf_op | source)
XLA Modules:
  0.0 153.5 jit_solution(11994128458922710513)
XLA Ops:
  0.0 5.3 %first.1 = (bf16[1040,256]{1,0:T(8,128)(2,1)}, bf16[1040,256]{1,0:T(8,128)(2,1)}, bf16[1040,256]{1,0:T(8,128)(2,1)}, bf16[1040,256]{1,0:T(8,128)(2,1)}, bf16[2,4...) custom-call(bf16[256,512]{1,0:T(8,128)(2,1)} %constant.10.clone.table_hbm, ...), custom_call_target="tpu_custom_call" | custom-call | tf_op jit(solution)/shard_map/first/pallas_call | solution.py:291
  5.4 15.7 %all-to-all-start = ((bf16[256,8,256]{2,1,0:T(8,128)(2,1)}), bf16[256,8,256]{2,1,0:T(8,128)(2,1)S(1)}, u32[]{:S(2)}, u32[]{:S(2)}) async-start(bf16[256,8,256]{2,1,0:T(8,128)(2,1)} %bitcast.2), calls=%async_computation | async-start | bytes 2097152 | tf_op jit(solution)/shard_map/all_to_all | solution.py:284
  21.0 1.4 collective-permute-start.9
  22.5 2.5 %collective-permute-start.11 = (bf16[1040,256]{1,0:T(8,128)(2,1)}, bf16[1040,256]{1,0:T(8,128)(2,1)S(1)}, u32[]{:S(2)}, u32[]{:S(2)}) collective-permute-start(bf16[1040,256]{1,0:T(8,128)(2,1)} %get-tuple-element.35), channel_id=1, source_target_pairs={{0,128},{64,192},{128,0},{192,64},{1,129},{65,193},{129,1},{193,65... | collective-permute-start | bytes 1597448 | tf_op jit(solution)/shard_map/ppermute | solution.py:288
  24.9 1.1 collective-permute-start.13
  26.0 1.2 collective-permute-start.8
  27.3 15.3 %collective-permute-done.9.rest_6_ = bf16[1040,256]{1,0:T(8,128)(2,1)S(1)} collective-permute-done((bf16[1040,256]{1,0:T(8,128)(2,1)}, bf16[1040,256]{1,0:T(8,128)(2,1)S(1)}, u32[]{:S(2)}, u32[]{:S(2)}) %collective-permute-start.9) | collective-permute-done | bytes 532512 | tf_op jit(solution)/shard_map/ppermute | solution.py:288
  42.6 3.1 %collective-permute-start.10 = (bf16[1040,256]{1,0:T(8,128)(2,1)S(1)}, bf16[1040,256]{1,0:T(8,128)(2,1)S(1)}, u32[]{:S(2)}, u32[]{:S(2)}) collective-permute-start(bf16[1040,256]{1,0:T(8,128)(2,1)S(1)} %collective-permute-done.9.rest_6_), channel_id=1, source_target_pairs={{0,32},{32,0},{1,33},{33,1},{2,34},{34,2},{3,35},{35,3},{4,36},{36... | collective-permute-start | bytes 1597448 | tf_op jit(solution)/shard_map/ppermute | solution.py:288
  45.7 13.4 %collective-permute-done.11.rest_8_ = bf16[1040,256]{1,0:T(8,128)(2,1)S(1)} collective-permute-done((bf16[1040,256]{1,0:T(8,128)(2,1)}, bf16[1040,256]{1,0:T(8,128)(2,1)S(1)}, u32[]{:S(2)}, u32[]{:S(2)}) %collective-permute-start.11) | collective-permute-done | bytes 532512 | tf_op jit(solution)/shard_map/ppermute | solution.py:288
  59.0 0.9 collective-permute-start.12
  60.1 7.4 %collective-permute-start = (bf16[2,4,4,8,256]{4,3,2,1,0:T(8,128)(2,1)S(1)}, bf16[2,4,4,8,256]{4,3,2,1,0:T(8,128)(2,1)S(1)}, u32[]{:S(2)}, u32[]{:S(2)}) collective-permute-start(bf16[2,4,4,8,256]{4,3,2,1,0:T(8,128)(2,1)S(1)} %get-tuple-element.22), channel_id=1, source_target_pairs={{0,0},{1,1},{2,2},{3,3},{4,4},{5,5},{6,6},{7,7},{32,36},{33,37},{3... | collective-permute-start | bytes 393224 | tf_op jit(solution)/shard_map/ppermute | solution.py:323
  67.5 2.4 %collective-permute-done.arrived_ref = bf16[2,4,4,8,256]{4,3,2,1,0:T(8,128)(2,1)S(1)} collective-permute-done((bf16[2,4,4,8,256]{4,3,2,1,0:T(8,128)(2,1)S(1)}, bf16[2,4,4,8,256]{4,3,2,1,0:T(8,128)(2,1)S(1)}, u32[]{:S(2)}, u32[]{:S(2)}) %collective-permute-start) | collective-permute-done | bytes 131104 | tf_op jit(solution)/shard_map/ppermute | solution.py:323
  70.0 1.2 collective-permute-done.1.arrived_ref
  72.0 3.3 %collective-permute-done.2.refs_1_ = bf16[2,4,8,256]{3,2,1,0:T(8,128)(2,1)S(1)} collective-permute-done((bf16[2,4,8,256]{3,2,1,0:T(8,128)(2,1)S(1)}, bf16[2,4,8,256]{3,2,1,0:T(8,128)(2,1)S(1)}, u32[]{:S(2)}, u32[]{:S(2)}) %collective-permute-start.2) | collective-permute-done | bytes 32800 | tf_op jit(solution)/shard_map/ppermute | solution.py:288
  76.0 3.6 %collective-permute-done.3.refs_2_ = bf16[2,4,8,256]{3,2,1,0:T(8,128)(2,1)S(1)} collective-permute-done((bf16[2,4,8,256]{3,2,1,0:T(8,128)(2,1)S(1)}, bf16[2,4,8,256]{3,2,1,0:T(8,128)(2,1)S(1)}, u32[]{:S(2)}, u32[]{:S(2)}) %collective-permute-start.3) | collective-permute-done | bytes 32800 | tf_op jit(solution)/shard_map/ppermute | solution.py:288
  80.0 2.3 %collective-permute-done.4.refs_3_ = bf16[2,4,8,256]{3,2,1,0:T(8,128)(2,1)S(1)} collective-permute-done((bf16[2,4,8,256]{3,2,1,0:T(8,128)(2,1)S(1)}, bf16[2,4,8,256]{3,2,1,0:T(8,128)(2,1)S(1)}, u32[]{:S(2)}, u32[]{:S(2)}) %collective-permute-start.4) | collective-permute-done | bytes 32800 | tf_op jit(solution)/shard_map/ppermute | solution.py:288
  82.4 1.8 %collective-permute-start.5 = (bf16[4,2,8,256]{3,2,1,0:T(8,128)(2,1)S(1)}, bf16[4,2,8,256]{3,2,1,0:T(8,128)(2,1)S(1)}, u32[]{:S(2)}, u32[]{:S(2)}) collective-permute-start(bf16[4,2,8,256]{3,2,1,0:T(8,128)(2,1)S(1)} %get-tuple-element.30), channel_id=1, source_target_pairs={{0,64},{64,128},{128,192},{192,0},{1,65},{65,129},{129,193},{193,1... | collective-permute-start | bytes 98312 | tf_op jit(solution)/shard_map/ppermute | solution.py:288
  84.2 2.3 %collective-permute-done.5.rest_1_ = bf16[4,2,8,256]{3,2,1,0:T(8,128)(2,1)S(1)} collective-permute-done((bf16[4,2,8,256]{3,2,1,0:T(8,128)(2,1)S(1)}, bf16[4,2,8,256]{3,2,1,0:T(8,128)(2,1)S(1)}, u32[]{:S(2)}, u32[]{:S(2)}) %collective-permute-start.5) | collective-permute-done | bytes 32800 | tf_op jit(solution)/shard_map/ppermute | solution.py:288
  86.4 0.8 collective-permute-start.6
  87.3 3.6 %collective-permute-done.6.rest_2_ = bf16[4,2,8,256]{3,2,1,0:T(8,128)(2,1)S(1)} collective-permute-done((bf16[4,2,8,256]{3,2,1,0:T(8,128)(2,1)S(1)}, bf16[4,2,8,256]{3,2,1,0:T(8,128)(2,1)S(1)}, u32[]{:S(2)}, u32[]{:S(2)}) %collective-permute-start.6) | collective-permute-done | bytes 32800 | tf_op jit(solution)/shard_map/ppermute | solution.py:288
  90.9 2.8 %collective-permute-done.7.rest_3_ = bf16[4,2,8,256]{3,2,1,0:T(8,128)(2,1)S(1)} collective-permute-done((bf16[4,2,8,256]{3,2,1,0:T(8,128)(2,1)S(1)}, bf16[4,2,8,256]{3,2,1,0:T(8,128)(2,1)S(1)}, u32[]{:S(2)}, u32[]{:S(2)}) %collective-permute-start.7) | collective-permute-done | bytes 32800 | tf_op jit(solution)/shard_map/ppermute | solution.py:288
  95.6 8.5 %chain.1 = bf16[8,2,2,2,4,8,256]{6,5,4,3,2,1,0:T(8,128)(2,1)S(1)} custom-call(bf16[8,2,2,2,4,8,256]{6,5,4,3,2,1,0:T(8,128)(2,1)S(1)} %bitcast.9, bf16[256,512]{1,0:T(8,128)(2,1)S(1)} %copy-done.3, bf16[256,512]{1,0:T(8,128)(2,1)S(1)} %copy-done.2, bf16[2,256,256]{2,1,0:T(8,128)(2,1)S(1)} %copy-done.1, bf16[4,2,8,256]{3,2,1,0:T(8,128)(2,1)S(1)} %get-tuple-element.29.rest_0_, ...), custom_call_target="tpu_custom_call" | custom-call | tf_op jit(solution)/shard_map/chain/pallas_call | solution.py:358
  104.1 47.7 %all_to_all.10 = bf16[256,8,256]{2,1,0:T(8,128)(2,1)S(1)} all-to-all(bf16[256,8,256]{2,1,0:T(8,128)(2,1)S(1)} %bitcast.10), channel_id=1, replica_groups=mesh['y'=4,'core'=2,'x'=4,'z'=8] {'z','core','x','y'}, dimensions={0} | all-to-all | bytes 2097152 | tf_op jit(solution)/shard_map/all_to_all | solution.py:284
  151.8 1.5 %inverse_rows.1 = bf16[256,2048]{1,0:T(8,128)(2,1)} custom-call(bf16[256,512]{1,0:T(8,128)(2,1)S(1)} %copy-done.4, bf16[8,2,2,2,4,8,256]{6,5,4,3,2,1,0:T(8,128)(2,1)S(1)} %bitcast.11, bf16[256,2048]{1,0:T(8,128)(2,1)S(1)} %bitcast.8), custom_call_target="tpu_custom_call" | custom-call | tf_op jit(solution)/shard_map/inverse_rows/pallas_call | solution.py:371
  (39 shorter events, 4.0 us)
Async XLA Ops:
  5.3 90.2 %copy-start.1 = (bf16[2,256,256]{2,1,0:T(8,128)(2,1)S(1)}, bf16[2,256,256]{2,1,0:T(8,128)(2,1)}, u32[]{:S(2)}) copy-start(bf16[2,256,256]{2,1,0:T(8,128)(2,1)} %constant.13.clone.fold_ref) | copy-start | bytes 786436
  5.3 90.2 %copy-start.2 = (bf16[256,512]{1,0:T(8,128)(2,1)S(1)}, bf16[256,512]{1,0:T(8,128)(2,1)}, u32[]{:S(2)}) copy-start(bf16[256,512]{1,0:T(8,128)(2,1)} %constant.12.clone.inv_ref) | copy-start | bytes 786436
  5.3 90.2 %copy-start.3 = (bf16[256,512]{1,0:T(8,128)(2,1)S(1)}, bf16[256,512]{1,0:T(8,128)(2,1)}, u32[]{:S(2)}) copy-start(bf16[256,512]{1,0:T(8,128)(2,1)} %constant.11.clone.col_ref) | copy-start | bytes 786436
  5.4 90.2 %all-to-all-start = ((bf16[256,8,256]{2,1,0:T(8,128)(2,1)}), bf16[256,8,256]{2,1,0:T(8,128)(2,1)S(1)}, u32[]{:S(2)}, u32[]{:S(2)}) async-start(bf16[256,8,256]{2,1,0:T(8,128)(2,1)} %bitcast.2), calls=%async_computation | async-start | bytes 2097152 | tf_op jit(solution)/shard_map/all_to_all | solution.py:284
  21.0 21.5 %collective-permute-start.9 = (bf16[1040,256]{1,0:T(8,128)(2,1)}, bf16[1040,256]{1,0:T(8,128)(2,1)S(1)}, u32[]{:S(2)}, u32[]{:S(2)}) collective-permute-start(bf16[1040,256]{1,0:T(8,128)(2,1)} %get-tuple-element.34), channel_id=1, source_target_pairs={{0,64},{64,128},{128,192},{192,0},{1,65},{65,129},{129,193},{193,1... | collective-permute-start | bytes 1597448 | tf_op jit(solution)/shard_map/ppermute | solution.py:288
  22.5 36.6 %collective-permute-start.11 = (bf16[1040,256]{1,0:T(8,128)(2,1)}, bf16[1040,256]{1,0:T(8,128)(2,1)S(1)}, u32[]{:S(2)}, u32[]{:S(2)}) collective-permute-start(bf16[1040,256]{1,0:T(8,128)(2,1)} %get-tuple-element.35), channel_id=1, source_target_pairs={{0,128},{64,192},{128,0},{192,64},{1,129},{65,193},{129,1},{193,65... | collective-permute-start | bytes 1597448 | tf_op jit(solution)/shard_map/ppermute | solution.py:288
  24.9 35.1 %collective-permute-start.13 = (bf16[1040,256]{1,0:T(8,128)(2,1)}, bf16[1040,256]{1,0:T(8,128)(2,1)S(1)}, u32[]{:S(2)}, u32[]{:S(2)}) collective-permute-start(bf16[1040,256]{1,0:T(8,128)(2,1)} %get-tuple-element.36), channel_id=1, source_target_pairs={{0,192},{64,0},{128,64},{192,128},{1,193},{65,1},{129,65},{193,129... | collective-permute-start | bytes 1597448 | tf_op jit(solution)/shard_map/ppermute | solution.py:288
  26.0 67.7 %collective-permute-start.8 = (bf16[1040,256]{1,0:T(8,128)(2,1)S(1)}, bf16[1040,256]{1,0:T(8,128)(2,1)S(1)}, u32[]{:S(2)}, u32[]{:S(2)}) collective-permute-start(bf16[1040,256]{1,0:T(8,128)(2,1)S(1)} %copy-done.5), channel_id=1, source_target_pairs={{0,32},{32,0},{1,33},{33,1},{2,34},{34,2},{3,35},{35,3},{4,36},{36... | collective-permute-start | bytes 1597448 | tf_op jit(solution)/shard_map/ppermute | solution.py:288
  42.6 53.0 %copy-start.6 = (bf16[1040,256]{1,0:T(8,128)(2,1)}, bf16[1040,256]{1,0:T(8,128)(2,1)S(1)}, u32[]{:S(2)}) copy-start(bf16[1040,256]{1,0:T(8,128)(2,1)S(1)} %collective-permute-done.9.rest_6_) | copy-start | bytes 1597444
  42.6 51.2 %collective-permute-start.10 = (bf16[1040,256]{1,0:T(8,128)(2,1)S(1)}, bf16[1040,256]{1,0:T(8,128)(2,1)S(1)}, u32[]{:S(2)}, u32[]{:S(2)}) collective-permute-start(bf16[1040,256]{1,0:T(8,128)(2,1)S(1)} %collective-permute-done.9.rest_6_), channel_id=1, source_target_pairs={{0,32},{32,0},{1,33},{33,1},{2,34},{34,2},{3,35},{35,3},{4,36},{36... | collective-permute-start | bytes 1597448 | tf_op jit(solution)/shard_map/ppermute | solution.py:288
  59.0 34.7 %copy-start.7 = (bf16[1040,256]{1,0:T(8,128)(2,1)}, bf16[1040,256]{1,0:T(8,128)(2,1)S(1)}, u32[]{:S(2)}) copy-start(bf16[1040,256]{1,0:T(8,128)(2,1)S(1)} %collective-permute-done.11.rest_8_) | copy-start | bytes 1597444
  59.0 34.7 %collective-permute-start.12 = (bf16[1040,256]{1,0:T(8,128)(2,1)S(1)}, bf16[1040,256]{1,0:T(8,128)(2,1)S(1)}, u32[]{:S(2)}, u32[]{:S(2)}) collective-permute-start(bf16[1040,256]{1,0:T(8,128)(2,1)S(1)} %collective-permute-done.11.rest_8_), channel_id=1, source_target_pairs={{0,32},{32,0},{1,33},{33,1},{2,34},{34,2},{3,35},{35,3},{4,36},{36... | collective-permute-start | bytes 1597448 | tf_op jit(solution)/shard_map/ppermute | solution.py:288
  60.0 33.8 %copy-start.8 = (bf16[1040,256]{1,0:T(8,128)(2,1)}, bf16[1040,256]{1,0:T(8,128)(2,1)S(1)}, u32[]{:S(2)}) copy-start(bf16[1040,256]{1,0:T(8,128)(2,1)S(1)} %collective-permute-done.13.rest_10_) | copy-start | bytes 1597444
  60.0 35.6 %collective-permute-start.14 = (bf16[1040,256]{1,0:T(8,128)(2,1)S(1)}, bf16[1040,256]{1,0:T(8,128)(2,1)}, u32[]{:S(2)}, u32[]{:S(2)}) collective-permute-start(bf16[1040,256]{1,0:T(8,128)(2,1)S(1)} %collective-permute-done.13.rest_10_), channel_id=1, source_target_pairs={{0,32},{32,0},{1,33},{33,1},{2,34},{34,2},{3,35},{35,3},{4,36},{36... | collective-permute-start | bytes 1597448 | tf_op jit(solution)/shard_map/ppermute | solution.py:288
  60.1 9.8 %collective-permute-start = (bf16[2,4,4,8,256]{4,3,2,1,0:T(8,128)(2,1)S(1)}, bf16[2,4,4,8,256]{4,3,2,1,0:T(8,128)(2,1)S(1)}, u32[]{:S(2)}, u32[]{:S(2)}) collective-permute-start(bf16[2,4,4,8,256]{4,3,2,1,0:T(8,128)(2,1)S(1)} %get-tuple-element.22), channel_id=1, source_target_pairs={{0,0},{1,1},{2,2},{3,3},{4,4},{5,5},{6,6},{7,7},{32,36},{33,37},{3... | collective-permute-start | bytes 393224 | tf_op jit(solution)/shard_map/ppermute | solution.py:323
  69.9 1.3 collective-permute-start.1
  71.3 4.1 %collective-permute-start.2 = (bf16[2,4,8,256]{3,2,1,0:T(8,128)(2,1)S(1)}, bf16[2,4,8,256]{3,2,1,0:T(8,128)(2,1)S(1)}, u32[]{:S(2)}, u32[]{:S(2)}) collective-permute-start(bf16[2,4,8,256]{3,2,1,0:T(8,128)(2,1)S(1)} %get-tuple-element.26), channel_id=1, source_target_pairs={{0,8},{8,16},{16,24},{24,0},{1,9},{9,17},{17,25},{25,1},{2,10},{10... | collective-permute-start | bytes 98312 | tf_op jit(solution)/shard_map/ppermute | solution.py:288
  75.3 4.3 %collective-permute-start.3 = (bf16[2,4,8,256]{3,2,1,0:T(8,128)(2,1)S(1)}, bf16[2,4,8,256]{3,2,1,0:T(8,128)(2,1)S(1)}, u32[]{:S(2)}, u32[]{:S(2)}) collective-permute-start(bf16[2,4,8,256]{3,2,1,0:T(8,128)(2,1)S(1)} %get-tuple-element.27), channel_id=1, source_target_pairs={{0,16},{8,24},{16,0},{24,8},{1,17},{9,25},{17,1},{25,9},{2,18},{10... | collective-permute-start | bytes 98312 | tf_op jit(solution)/shard_map/ppermute | solution.py:288
  79.6 2.8 %collective-permute-start.4 = (bf16[2,4,8,256]{3,2,1,0:T(8,128)(2,1)S(1)}, bf16[2,4,8,256]{3,2,1,0:T(8,128)(2,1)S(1)}, u32[]{:S(2)}, u32[]{:S(2)}) collective-permute-start(bf16[2,4,8,256]{3,2,1,0:T(8,128)(2,1)S(1)} %get-tuple-element.28), channel_id=1, source_target_pairs={{0,24},{8,0},{16,8},{24,16},{1,25},{9,1},{17,9},{25,17},{2,26},{10... | collective-permute-start | bytes 98312 | tf_op jit(solution)/shard_map/ppermute | solution.py:288
  82.4 4.1 %collective-permute-start.5 = (bf16[4,2,8,256]{3,2,1,0:T(8,128)(2,1)S(1)}, bf16[4,2,8,256]{3,2,1,0:T(8,128)(2,1)S(1)}, u32[]{:S(2)}, u32[]{:S(2)}) collective-permute-start(bf16[4,2,8,256]{3,2,1,0:T(8,128)(2,1)S(1)} %get-tuple-element.30), channel_id=1, source_target_pairs={{0,64},{64,128},{128,192},{192,0},{1,65},{65,129},{129,193},{193,1... | collective-permute-start | bytes 98312 | tf_op jit(solution)/shard_map/ppermute | solution.py:288
  86.4 4.4 %collective-permute-start.6 = (bf16[4,2,8,256]{3,2,1,0:T(8,128)(2,1)S(1)}, bf16[4,2,8,256]{3,2,1,0:T(8,128)(2,1)S(1)}, u32[]{:S(2)}, u32[]{:S(2)}) collective-permute-start(bf16[4,2,8,256]{3,2,1,0:T(8,128)(2,1)S(1)} %get-tuple-element.31), channel_id=1, source_target_pairs={{0,128},{64,192},{128,0},{192,64},{1,129},{65,193},{129,1},{193,65... | collective-permute-start | bytes 98312 | tf_op jit(solution)/shard_map/ppermute | solution.py:288
  90.8 2.9 %collective-permute-start.7 = (bf16[4,2,8,256]{3,2,1,0:T(8,128)(2,1)S(1)}, bf16[4,2,8,256]{3,2,1,0:T(8,128)(2,1)S(1)}, u32[]{:S(2)}, u32[]{:S(2)}) collective-permute-start(bf16[4,2,8,256]{3,2,1,0:T(8,128)(2,1)S(1)} %get-tuple-element.32), channel_id=1, source_target_pairs={{0,192},{64,0},{128,64},{192,128},{1,193},{65,1},{129,65},{193,129... | collective-permute-start | bytes 98312 | tf_op jit(solution)/shard_map/ppermute | solution.py:288
  104.0 47.8 %copy-start = (bf16[2,128,2048]{2,1,0:T(8,128)(2,1)S(1)}, bf16[2,128,2048]{2,1,0:T(8,128)(2,1)}, u32[]{:S(2)}) copy-start(bf16[2,128,2048]{2,1,0:T(8,128)(2,1)} %param.11) | copy-start | bytes 3145732
  104.1 47.8 %copy-start.4 = (bf16[256,512]{1,0:T(8,128)(2,1)S(1)}, bf16[256,512]{1,0:T(8,128)(2,1)}, u32[]{:S(2)}) copy-start(bf16[256,512]{1,0:T(8,128)(2,1)} %constant.14.clone.table_ref) | copy-start | bytes 786436
  (4 other events, 23.3 us)

commit v2 on v1

--- a/solution.py
+++ b/solution.py
@@ -95,11 +95,6 @@
         (act_hbm, act_ref),
         (bias_hbm, biases),
     ]
-    own = []
-    for k, (source, place) in enumerate(pairs):
-        copy = pltpu.make_async_copy(source, place, own_sems.at[k])
-        copy.start()
-        own.append(copy)
     loads = []
     for d in range(Y):
         block = ((y + d) & (Y - 1)) * 2 + odd
@@ -112,6 +107,11 @@
                 )
                 copy.start()
                 loads.append(copy)
+    own = []
+    for k, (source, place) in enumerate(pairs):
+        copy = pltpu.make_async_copy(source, place, own_sems.at[k])
+        copy.start()
+        own.append(copy)
 
     depth = table_ref.shape[1] // 2
     line = lax.broadcasted_iota(jnp.int32, (lines, size), 0)
@@ -127,14 +127,8 @@
             for m in range(2):
                 cot_rows_ref[i, n // 2, 2 * m + n % 2] = tiles[(2 * i + m) * 8 : (2 * i + m + 1) * 8]
 
-    def transform(n):
-        spectrum = twice(table_ref, act_ref[:, n * size : (n + 1) * size]).astype(BF16)
-        rows_ref[:, :, :, n % 2, n // 2] = spectrum.reshape(Z, 2, 2, 8, size)
-
     for copy in own[2:]:
         copy.wait()
-    for n in range(3):
-        transform(n)
     for d in range(Y):
         block = ((y + d) & (Y - 1)) * 2 + odd
         bias = biases[0, :, pl.ds(block * size, size)]
@@ -143,15 +137,16 @@
         low = bias - high - middle
         packed = jnp.concatenate([high, middle, low, jnp.zeros((10, size), F32)], axis=0)
         held[d, 4 * size : 4 * size + 16] = packed.astype(BF16)
-    for copy in loads:
-        copy.wait()
     stores = []
     for d in range(Y):
+        for copy in loads[4 * d : 4 * d + 4]:
+            copy.wait()
         copy = pltpu.make_async_copy(held.at[d], pieces[d], sems.at[d, 4])
         copy.start()
         stores.append(copy)
-    for n in range(3, 2 * Y):
-        transform(n)
+    for n in range(2 * Y):
+        spectrum = twice(table_ref, act_ref[:, n * size : (n + 1) * size]).astype(BF16)
+        rows_ref[:, :, :, n % 2, n // 2] = spectrum.reshape(Z, 2, 2, 8, size)
     for copy in stores:
         copy.wait()
 

time: 154 us -> 154 us (level)
  no operation moved by 1% of the time
where the time goes in v2:
time: 154 us; the launch traced here: 153 us
  waiting for transfers between devices  50.2 us (33%)
  blocking collectives  47.8 us (31%)
  starting transfers between devices  38.1 us (25%)
  Pallas kernels  15 us (10%)
  local copies, waits for them, and re-layouts  1.8 us (1%)
    ppermute x14, waiting for transfers between devices, shifted(): lax.ppermute(value, axis, [(i, (i + distance) % size) for i in range(size)])  47.8 us
    all_to_all x1, blocking collectives, exchange(): lax.all_to_all(flat, EVERYONE, split_axis=0, concat_axis=0, tiled=True)  47.8 us
    all_to_all x1, starting transfers between devices, exchange(): lax.all_to_all(flat, EVERYONE, split_axis=0, concat_axis=0, tiled=True)  15.7 us
    ppermute x14, starting transfers between devices, shifted(): lax.ppermute(value, axis, [(i, (i + distance) % size) for i in range(size)])  15 us
    pallas_call x1, Pallas kernels, body(): pl.pallas_call(chain_kernel, in_specs=[vmem] * (4 + X) + [hbm] * sections...  8.47 us
    ppermute x1, starting transfers between devices, body(): arrived = lax.ppermute(cot_rows, ('y', 'core', 'z'), route)  7.38 us
    pallas_call x1, Pallas kernels, body(): pl.pallas_call(first_kernel, in_specs=[hbm] * 6, out_specs=[hbm] * Y + [v...  4.91 us
  transfers between devices with their start and end apart: 16, of which 10 were waited for; matrix products, arithmetic and copies ran while one was open for 0% of the time, Pallas kernels for 0%

profile of v2, /device:TPU:1, one launch (start us, length us, event | category | flops | bytes accessed | tf_op | source)
XLA Modules:
  0.0 153.2 jit_solution(6999966604243094523)
XLA Ops:
  0.0 4.9 %first.1 = (bf16[1040,256]{1,0:T(8,128)(2,1)}, bf16[1040,256]{1,0:T(8,128)(2,1)}, bf16[1040,256]{1,0:T(8,128)(2,1)}, bf16[1040,256]{1,0:T(8,128)(2,1)}, bf16[2,4...) custom-call(bf16[256,512]{1,0:T(8,128)(2,1)} %constant.10.clone.table_hbm, ...), custom_call_target="tpu_custom_call" | custom-call | tf_op jit(solution)/shard_map/first/pallas_call | solution.py:286
  5.0 15.7 %all-to-all-start = ((bf16[256,8,256]{2,1,0:T(8,128)(2,1)}), bf16[256,8,256]{2,1,0:T(8,128)(2,1)S(1)}, u32[]{:S(2)}, u32[]{:S(2)}) async-start(bf16[256,8,256]{2,1,0:T(8,128)(2,1)} %bitcast.2), calls=%async_computation | async-start | bytes 2097152 | tf_op jit(solution)/shard_map/all_to_all | solution.py:279
  20.6 1.4 collective-permute-start.9
  22.1 2.5 %collective-permute-start.11 = (bf16[1040,256]{1,0:T(8,128)(2,1)}, bf16[1040,256]{1,0:T(8,128)(2,1)S(1)}, u32[]{:S(2)}, u32[]{:S(2)}) collective-permute-start(bf16[1040,256]{1,0:T(8,128)(2,1)} %get-tuple-element.35), channel_id=1, source_target_pairs={{0,128},{64,192},{128,0},{192,64},{1,129},{65,193},{129,1},{193,65... | collective-permute-start | bytes 1597448 | tf_op jit(solution)/shard_map/ppermute | solution.py:283
  24.5 1.1 collective-permute-start.13
  25.6 1.2 collective-permute-start.8
  26.9 15.3 %collective-permute-done.9.rest_6_ = bf16[1040,256]{1,0:T(8,128)(2,1)S(1)} collective-permute-done((bf16[1040,256]{1,0:T(8,128)(2,1)}, bf16[1040,256]{1,0:T(8,128)(2,1)S(1)}, u32[]{:S(2)}, u32[]{:S(2)}) %collective-permute-start.9) | collective-permute-done | bytes 532512 | tf_op jit(solution)/shard_map/ppermute | solution.py:283
  42.2 3.1 %collective-permute-start.10 = (bf16[1040,256]{1,0:T(8,128)(2,1)S(1)}, bf16[1040,256]{1,0:T(8,128)(2,1)S(1)}, u32[]{:S(2)}, u32[]{:S(2)}) collective-permute-start(bf16[1040,256]{1,0:T(8,128)(2,1)S(1)} %collective-permute-done.9.rest_6_), channel_id=1, source_target_pairs={{0,32},{32,0},{1,33},{33,1},{2,34},{34,2},{3,35},{35,3},{4,36},{36... | collective-permute-start | bytes 1597448 | tf_op jit(solution)/shard_map/ppermute | solution.py:283
  45.3 13.4 %collective-permute-done.11.rest_8_ = bf16[1040,256]{1,0:T(8,128)(2,1)S(1)} collective-permute-done((bf16[1040,256]{1,0:T(8,128)(2,1)}, bf16[1040,256]{1,0:T(8,128)(2,1)S(1)}, u32[]{:S(2)}, u32[]{:S(2)}) %collective-permute-start.11) | collective-permute-done | bytes 532512 | tf_op jit(solution)/shard_map/ppermute | solution.py:283
  58.7 0.9 collective-permute-start.12
  59.7 7.4 %collective-permute-start = (bf16[2,4,4,8,256]{4,3,2,1,0:T(8,128)(2,1)S(1)}, bf16[2,4,4,8,256]{4,3,2,1,0:T(8,128)(2,1)S(1)}, u32[]{:S(2)}, u32[]{:S(2)}) collective-permute-start(bf16[2,4,4,8,256]{4,3,2,1,0:T(8,128)(2,1)S(1)} %get-tuple-element.22), channel_id=1, source_target_pairs={{0,0},{1,1},{2,2},{3,3},{4,4},{5,5},{6,6},{7,7},{32,36},{33,37},{3... | collective-permute-start | bytes 393224 | tf_op jit(solution)/shard_map/ppermute | solution.py:318
  67.1 2.4 %collective-permute-done.arrived_ref = bf16[2,4,4,8,256]{4,3,2,1,0:T(8,128)(2,1)S(1)} collective-permute-done((bf16[2,4,4,8,256]{4,3,2,1,0:T(8,128)(2,1)S(1)}, bf16[2,4,4,8,256]{4,3,2,1,0:T(8,128)(2,1)S(1)}, u32[]{:S(2)}, u32[]{:S(2)}) %collective-permute-start) | collective-permute-done | bytes 131104 | tf_op jit(solution)/shard_map/ppermute | solution.py:318
  69.6 1.2 collective-permute-done.1.arrived_ref
  71.7 3.3 %collective-permute-done.2.refs_1_ = bf16[2,4,8,256]{3,2,1,0:T(8,128)(2,1)S(1)} collective-permute-done((bf16[2,4,8,256]{3,2,1,0:T(8,128)(2,1)S(1)}, bf16[2,4,8,256]{3,2,1,0:T(8,128)(2,1)S(1)}, u32[]{:S(2)}, u32[]{:S(2)}) %collective-permute-start.2) | collective-permute-done | bytes 32800 | tf_op jit(solution)/shard_map/ppermute | solution.py:283
  75.6 3.6 %collective-permute-done.3.refs_2_ = bf16[2,4,8,256]{3,2,1,0:T(8,128)(2,1)S(1)} collective-permute-done((bf16[2,4,8,256]{3,2,1,0:T(8,128)(2,1)S(1)}, bf16[2,4,8,256]{3,2,1,0:T(8,128)(2,1)S(1)}, u32[]{:S(2)}, u32[]{:S(2)}) %collective-permute-start.3) | collective-permute-done | bytes 32800 | tf_op jit(solution)/shard_map/ppermute | solution.py:283
  79.6 2.3 %collective-permute-done.4.refs_3_ = bf16[2,4,8,256]{3,2,1,0:T(8,128)(2,1)S(1)} collective-permute-done((bf16[2,4,8,256]{3,2,1,0:T(8,128)(2,1)S(1)}, bf16[2,4,8,256]{3,2,1,0:T(8,128)(2,1)S(1)}, u32[]{:S(2)}, u32[]{:S(2)}) %collective-permute-start.4) | collective-permute-done | bytes 32800 | tf_op jit(solution)/shard_map/ppermute | solution.py:283
  82.0 1.8 %collective-permute-start.5 = (bf16[4,2,8,256]{3,2,1,0:T(8,128)(2,1)S(1)}, bf16[4,2,8,256]{3,2,1,0:T(8,128)(2,1)S(1)}, u32[]{:S(2)}, u32[]{:S(2)}) collective-permute-start(bf16[4,2,8,256]{3,2,1,0:T(8,128)(2,1)S(1)} %get-tuple-element.30), channel_id=1, source_target_pairs={{0,64},{64,128},{128,192},{192,0},{1,65},{65,129},{129,193},{193,1... | collective-permute-start | bytes 98312 | tf_op jit(solution)/shard_map/ppermute | solution.py:283
  83.8 2.3 %collective-permute-done.5.rest_1_ = bf16[4,2,8,256]{3,2,1,0:T(8,128)(2,1)S(1)} collective-permute-done((bf16[4,2,8,256]{3,2,1,0:T(8,128)(2,1)S(1)}, bf16[4,2,8,256]{3,2,1,0:T(8,128)(2,1)S(1)}, u32[]{:S(2)}, u32[]{:S(2)}) %collective-permute-start.5) | collective-permute-done | bytes 32800 | tf_op jit(solution)/shard_map/ppermute | solution.py:283
  86.0 0.8 collective-permute-start.6
  86.9 3.6 %collective-permute-done.6.rest_2_ = bf16[4,2,8,256]{3,2,1,0:T(8,128)(2,1)S(1)} collective-permute-done((bf16[4,2,8,256]{3,2,1,0:T(8,128)(2,1)S(1)}, bf16[4,2,8,256]{3,2,1,0:T(8,128)(2,1)S(1)}, u32[]{:S(2)}, u32[]{:S(2)}) %collective-permute-start.6) | collective-permute-done | bytes 32800 | tf_op jit(solution)/shard_map/ppermute | solution.py:283
  90.5 2.8 %collective-permute-done.7.rest_3_ = bf16[4,2,8,256]{3,2,1,0:T(8,128)(2,1)S(1)} collective-permute-done((bf16[4,2,8,256]{3,2,1,0:T(8,128)(2,1)S(1)}, bf16[4,2,8,256]{3,2,1,0:T(8,128)(2,1)S(1)}, u32[]{:S(2)}, u32[]{:S(2)}) %collective-permute-start.7) | collective-permute-done | bytes 32800 | tf_op jit(solution)/shard_map/ppermute | solution.py:283
  95.2 8.5 %chain.1 = bf16[8,2,2,2,4,8,256]{6,5,4,3,2,1,0:T(8,128)(2,1)S(1)} custom-call(bf16[8,2,2,2,4,8,256]{6,5,4,3,2,1,0:T(8,128)(2,1)S(1)} %bitcast.9, bf16[256,512]{1,0:T(8,128)(2,1)S(1)} %copy-done.3, bf16[256,512]{1,0:T(8,128)(2,1)S(1)} %copy-done.2, bf16[2,256,256]{2,1,0:T(8,128)(2,1)S(1)} %copy-done.1, bf16[4,2,8,256]{3,2,1,0:T(8,128)(2,1)S(1)} %get-tuple-element.29.rest_0_, ...), custom_call_target="tpu_custom_call" | custom-call | tf_op jit(solution)/shard_map/chain/pallas_call | solution.py:353
  103.7 47.8 %all_to_all.10 = bf16[256,8,256]{2,1,0:T(8,128)(2,1)S(1)} all-to-all(bf16[256,8,256]{2,1,0:T(8,128)(2,1)S(1)} %bitcast.10), channel_id=1, replica_groups=mesh['y'=4,'core'=2,'x'=4,'z'=8] {'z','core','x','y'}, dimensions={0} | all-to-all | bytes 2097152 | tf_op jit(solution)/shard_map/all_to_all | solution.py:279
  151.4 1.6 %inverse_rows.1 = bf16[256,2048]{1,0:T(8,128)(2,1)} custom-call(bf16[256,512]{1,0:T(8,128)(2,1)S(1)} %copy-done.4, bf16[8,2,2,2,4,8,256]{6,5,4,3,2,1,0:T(8,128)(2,1)S(1)} %bitcast.11, bf16[256,2048]{1,0:T(8,128)(2,1)S(1)} %bitcast.8), custom_call_target="tpu_custom_call" | custom-call | tf_op jit(solution)/shard_map/inverse_rows/pallas_call | solution.py:366
  (39 shorter events, 4.0 us)
Async XLA Ops:
  4.9 90.2 %copy-start.1 = (bf16[2,256,256]{2,1,0:T(8,128)(2,1)S(1)}, bf16[2,256,256]{2,1,0:T(8,128)(2,1)}, u32[]{:S(2)}) copy-start(bf16[2,256,256]{2,1,0:T(8,128)(2,1)} %constant.13.clone.fold_ref) | copy-start | bytes 786436
  4.9 90.2 %copy-start.2 = (bf16[256,512]{1,0:T(8,128)(2,1)S(1)}, bf16[256,512]{1,0:T(8,128)(2,1)}, u32[]{:S(2)}) copy-start(bf16[256,512]{1,0:T(8,128)(2,1)} %constant.12.clone.inv_ref) | copy-start | bytes 786436
  5.0 90.2 %copy-start.3 = (bf16[256,512]{1,0:T(8,128)(2,1)S(1)}, bf16[256,512]{1,0:T(8,128)(2,1)}, u32[]{:S(2)}) copy-start(bf16[256,512]{1,0:T(8,128)(2,1)} %constant.11.clone.col_ref) | copy-start | bytes 786436
  5.0 90.2 %all-to-all-start = ((bf16[256,8,256]{2,1,0:T(8,128)(2,1)}), bf16[256,8,256]{2,1,0:T(8,128)(2,1)S(1)}, u32[]{:S(2)}, u32[]{:S(2)}) async-start(bf16[256,8,256]{2,1,0:T(8,128)(2,1)} %bitcast.2), calls=%async_computation | async-start | bytes 2097152 | tf_op jit(solution)/shard_map/all_to_all | solution.py:279
  20.6 21.5 %collective-permute-start.9 = (bf16[1040,256]{1,0:T(8,128)(2,1)}, bf16[1040,256]{1,0:T(8,128)(2,1)S(1)}, u32[]{:S(2)}, u32[]{:S(2)}) collective-permute-start(bf16[1040,256]{1,0:T(8,128)(2,1)} %get-tuple-element.34), channel_id=1, source_target_pairs={{0,64},{64,128},{128,192},{192,0},{1,65},{65,129},{129,193},{193,1... | collective-permute-start | bytes 1597448 | tf_op jit(solution)/shard_map/ppermute | solution.py:283
  22.1 36.6 %collective-permute-start.11 = (bf16[1040,256]{1,0:T(8,128)(2,1)}, bf16[1040,256]{1,0:T(8,128)(2,1)S(1)}, u32[]{:S(2)}, u32[]{:S(2)}) collective-permute-start(bf16[1040,256]{1,0:T(8,128)(2,1)} %get-tuple-element.35), channel_id=1, source_target_pairs={{0,128},{64,192},{128,0},{192,64},{1,129},{65,193},{129,1},{193,65... | collective-permute-start | bytes 1597448 | tf_op jit(solution)/shard_map/ppermute | solution.py:283
  24.5 35.1 %collective-permute-start.13 = (bf16[1040,256]{1,0:T(8,128)(2,1)}, bf16[1040,256]{1,0:T(8,128)(2,1)S(1)}, u32[]{:S(2)}, u32[]{:S(2)}) collective-permute-start(bf16[1040,256]{1,0:T(8,128)(2,1)} %get-tuple-element.36), channel_id=1, source_target_pairs={{0,192},{64,0},{128,64},{192,128},{1,193},{65,1},{129,65},{193,129... | collective-permute-start | bytes 1597448 | tf_op jit(solution)/shard_map/ppermute | solution.py:283
  25.6 67.7 %collective-permute-start.8 = (bf16[1040,256]{1,0:T(8,128)(2,1)S(1)}, bf16[1040,256]{1,0:T(8,128)(2,1)S(1)}, u32[]{:S(2)}, u32[]{:S(2)}) collective-permute-start(bf16[1040,256]{1,0:T(8,128)(2,1)S(1)} %copy-done.5), channel_id=1, source_target_pairs={{0,32},{32,0},{1,33},{33,1},{2,34},{34,2},{3,35},{35,3},{4,36},{36... | collective-permute-start | bytes 1597448 | tf_op jit(solution)/shard_map/ppermute | solution.py:283
  42.2 53.0 %copy-start.6 = (bf16[1040,256]{1,0:T(8,128)(2,1)}, bf16[1040,256]{1,0:T(8,128)(2,1)S(1)}, u32[]{:S(2)}) copy-start(bf16[1040,256]{1,0:T(8,128)(2,1)S(1)} %collective-permute-done.9.rest_6_) | copy-start | bytes 1597444
  42.2 51.2 %collective-permute-start.10 = (bf16[1040,256]{1,0:T(8,128)(2,1)S(1)}, bf16[1040,256]{1,0:T(8,128)(2,1)S(1)}, u32[]{:S(2)}, u32[]{:S(2)}) collective-permute-start(bf16[1040,256]{1,0:T(8,128)(2,1)S(1)} %collective-permute-done.9.rest_6_), channel_id=1, source_target_pairs={{0,32},{32,0},{1,33},{33,1},{2,34},{34,2},{3,35},{35,3},{4,36},{36... | collective-permute-start | bytes 1597448 | tf_op jit(solution)/shard_map/ppermute | solution.py:283
  58.7 34.7 %copy-start.7 = (bf16[1040,256]{1,0:T(8,128)(2,1)}, bf16[1040,256]{1,0:T(8,128)(2,1)S(1)}, u32[]{:S(2)}) copy-start(bf16[1040,256]{1,0:T(8,128)(2,1)S(1)} %collective-permute-done.11.rest_8_) | copy-start | bytes 1597444
  58.7 34.7 %collective-permute-start.12 = (bf16[1040,256]{1,0:T(8,128)(2,1)S(1)}, bf16[1040,256]{1,0:T(8,128)(2,1)S(1)}, u32[]{:S(2)}, u32[]{:S(2)}) collective-permute-start(bf16[1040,256]{1,0:T(8,128)(2,1)S(1)} %collective-permute-done.11.rest_8_), channel_id=1, source_target_pairs={{0,32},{32,0},{1,33},{33,1},{2,34},{34,2},{3,35},{35,3},{4,36},{36... | collective-permute-start | bytes 1597448 | tf_op jit(solution)/shard_map/ppermute | solution.py:283
  59.6 33.8 %copy-start.8 = (bf16[1040,256]{1,0:T(8,128)(2,1)}, bf16[1040,256]{1,0:T(8,128)(2,1)S(1)}, u32[]{:S(2)}) copy-start(bf16[1040,256]{1,0:T(8,128)(2,1)S(1)} %collective-permute-done.13.rest_10_) | copy-start | bytes 1597444
  59.6 35.6 %collective-permute-start.14 = (bf16[1040,256]{1,0:T(8,128)(2,1)S(1)}, bf16[1040,256]{1,0:T(8,128)(2,1)}, u32[]{:S(2)}, u32[]{:S(2)}) collective-permute-start(bf16[1040,256]{1,0:T(8,128)(2,1)S(1)} %collective-permute-done.13.rest_10_), channel_id=1, source_target_pairs={{0,32},{32,0},{1,33},{33,1},{2,34},{34,2},{3,35},{35,3},{4,36},{36... | collective-permute-start | bytes 1597448 | tf_op jit(solution)/shard_map/ppermute | solution.py:283
  59.7 9.8 %collective-permute-start = (bf16[2,4,4,8,256]{4,3,2,1,0:T(8,128)(2,1)S(1)}, bf16[2,4,4,8,256]{4,3,2,1,0:T(8,128)(2,1)S(1)}, u32[]{:S(2)}, u32[]{:S(2)}) collective-permute-start(bf16[2,4,4,8,256]{4,3,2,1,0:T(8,128)(2,1)S(1)} %get-tuple-element.22), channel_id=1, source_target_pairs={{0,0},{1,1},{2,2},{3,3},{4,4},{5,5},{6,6},{7,7},{32,36},{33,37},{3... | collective-permute-start | bytes 393224 | tf_op jit(solution)/shard_map/ppermute | solution.py:318
  69.5 1.3 collective-permute-start.1
  70.9 4.1 %collective-permute-start.2 = (bf16[2,4,8,256]{3,2,1,0:T(8,128)(2,1)S(1)}, bf16[2,4,8,256]{3,2,1,0:T(8,128)(2,1)S(1)}, u32[]{:S(2)}, u32[]{:S(2)}) collective-permute-start(bf16[2,4,8,256]{3,2,1,0:T(8,128)(2,1)S(1)} %get-tuple-element.26), channel_id=1, source_target_pairs={{0,8},{8,16},{16,24},{24,0},{1,9},{9,17},{17,25},{25,1},{2,10},{10... | collective-permute-start | bytes 98312 | tf_op jit(solution)/shard_map/ppermute | solution.py:283
  74.9 4.3 %collective-permute-start.3 = (bf16[2,4,8,256]{3,2,1,0:T(8,128)(2,1)S(1)}, bf16[2,4,8,256]{3,2,1,0:T(8,128)(2,1)S(1)}, u32[]{:S(2)}, u32[]{:S(2)}) collective-permute-start(bf16[2,4,8,256]{3,2,1,0:T(8,128)(2,1)S(1)} %get-tuple-element.27), channel_id=1, source_target_pairs={{0,16},{8,24},{16,0},{24,8},{1,17},{9,25},{17,1},{25,9},{2,18},{10... | collective-permute-start | bytes 98312 | tf_op jit(solution)/shard_map/ppermute | solution.py:283
  79.2 2.8 %collective-permute-start.4 = (bf16[2,4,8,256]{3,2,1,0:T(8,128)(2,1)S(1)}, bf16[2,4,8,256]{3,2,1,0:T(8,128)(2,1)S(1)}, u32[]{:S(2)}, u32[]{:S(2)}) collective-permute-start(bf16[2,4,8,256]{3,2,1,0:T(8,128)(2,1)S(1)} %get-tuple-element.28), channel_id=1, source_target_pairs={{0,24},{8,0},{16,8},{24,16},{1,25},{9,1},{17,9},{25,17},{2,26},{10... | collective-permute-start | bytes 98312 | tf_op jit(solution)/shard_map/ppermute | solution.py:283
  82.0 4.1 %collective-permute-start.5 = (bf16[4,2,8,256]{3,2,1,0:T(8,128)(2,1)S(1)}, bf16[4,2,8,256]{3,2,1,0:T(8,128)(2,1)S(1)}, u32[]{:S(2)}, u32[]{:S(2)}) collective-permute-start(bf16[4,2,8,256]{3,2,1,0:T(8,128)(2,1)S(1)} %get-tuple-element.30), channel_id=1, source_target_pairs={{0,64},{64,128},{128,192},{192,0},{1,65},{65,129},{129,193},{193,1... | collective-permute-start | bytes 98312 | tf_op jit(solution)/shard_map/ppermute | solution.py:283
  86.0 4.4 %collective-permute-start.6 = (bf16[4,2,8,256]{3,2,1,0:T(8,128)(2,1)S(1)}, bf16[4,2,8,256]{3,2,1,0:T(8,128)(2,1)S(1)}, u32[]{:S(2)}, u32[]{:S(2)}) collective-permute-start(bf16[4,2,8,256]{3,2,1,0:T(8,128)(2,1)S(1)} %get-tuple-element.31), channel_id=1, source_target_pairs={{0,128},{64,192},{128,0},{192,64},{1,129},{65,193},{129,1},{193,65... | collective-permute-start | bytes 98312 | tf_op jit(solution)/shard_map/ppermute | solution.py:283
  90.4 2.9 %collective-permute-start.7 = (bf16[4,2,8,256]{3,2,1,0:T(8,128)(2,1)S(1)}, bf16[4,2,8,256]{3,2,1,0:T(8,128)(2,1)S(1)}, u32[]{:S(2)}, u32[]{:S(2)}) collective-permute-start(bf16[4,2,8,256]{3,2,1,0:T(8,128)(2,1)S(1)} %get-tuple-element.32), channel_id=1, source_target_pairs={{0,192},{64,0},{128,64},{192,128},{1,193},{65,1},{129,65},{193,129... | collective-permute-start | bytes 98312 | tf_op jit(solution)/shard_map/ppermute | solution.py:283
  103.7 47.8 %copy-start = (bf16[2,128,2048]{2,1,0:T(8,128)(2,1)S(1)}, bf16[2,128,2048]{2,1,0:T(8,128)(2,1)}, u32[]{:S(2)}) copy-start(bf16[2,128,2048]{2,1,0:T(8,128)(2,1)} %param.11) | copy-start | bytes 3145732
  103.7 47.8 %copy-start.4 = (bf16[256,512]{1,0:T(8,128)(2,1)S(1)}, bf16[256,512]{1,0:T(8,128)(2,1)}, u32[]{:S(2)}) copy-start(bf16[256,512]{1,0:T(8,128)(2,1)} %constant.14.clone.table_ref) | copy-start | bytes 786436
  (4 other events, 23.3 us)
